TPU v7x, 128 devices: a whole 4x4x4 slice. The times are simulated.
128 devices in a mesh: pole: 8 (over z, core), lat: 16 (over x, y).
Axes of the slice: x: 4, y: 4, z: 4, core: 2. Of those that a mesh axis runs over, the one named last changes fastest.
Arguments:
- fields: bfloat16 [8, 3, 1280, 2560], P(None, None, ('pole', 'lat')), may hold values from -6 to 6
- cycle_weights: float32 [1280], P(('pole', 'lat')), may hold values from 0.5 to 2
- legendre: bfloat16 [1280, 640, 1281], P(None, ('pole', 'lat')), may hold values from -0.15625 to 0.15625
- inverses: float32 [2, 8, 640, 2, 3, 3, 1281], P(None, None, ('pole', 'lat')), may hold values from -0.4 to 1
- pole_coeffs: float32 [2, 2], replicated, may hold values from -3 to 3
- pair_order: int32 [640], replicated, may hold values from 0 to 639, each once
Outputs:
- result: float32 [8, 3, 1280, 2560], P(None, None, ('pole', 'lat'))
Inputs may be any that keep to these rules, and one draw needn't show every extreme that they name: `pair_order`: each pair index appears once.
All inputs are finite; a program needn't handle non-finite values.
Results may differ from a plain program's by a relative error of at most 0.015.
Values may be sent and summed in bfloat16 or wider, within the bound.
No kernel may reach another device: no remote copies, remote signals or barrier semaphores. Data moves between devices by JAX's collectives and lax.ppermute only.
A program may use at most 192 MiB of HBM per device.

v0:
```python
import math

import jax
import jax.numpy as jnp
from jax import lax
from jax.sharding import PartitionSpec as P

ITERS = 3


ROTATION = 0.4
PRECISE = lax.Precision.HIGHEST


def coupling_weights(first_pair, wave_count, length):
    offset = jnp.arange(length, dtype=jnp.int32)
    base_pair = first_pair[..., None]
    in_first = offset < wave_count - base_pair
    order_int = jnp.where(in_first, base_pair, wave_count - 1 - base_pair)
    degree = jnp.where(in_first, base_pair + offset, offset - 1)
    order_m = order_int.astype(jnp.float32)
    lower_n = degree.astype(jnp.float32)
    upper_n = lower_n + 1.0
    down_ratio = jnp.maximum(lower_n * lower_n - order_m * order_m, 0.0) / jnp.maximum(
        4.0 * lower_n * lower_n - 1.0, 1.0
    )
    up_ratio = jnp.maximum(upper_n * upper_n - order_m * order_m, 0.0) / (
        4.0 * upper_n * upper_n - 1.0
    )
    eps_down = jnp.where(degree > order_int, ROTATION * jnp.sqrt(down_ratio), 0.0)
    eps_up = jnp.where(degree + 1 < wave_count, ROTATION * jnp.sqrt(up_ratio), 0.0)
    return (in_first, eps_down, eps_up)


def shift_prev(values):
    return jnp.concatenate([jnp.zeros_like(values[..., :1]), values[..., :-1]], axis=-1)


def shift_next(values):
    return jnp.concatenate([values[..., 1:], jnp.zeros_like(values[..., :1])], axis=-1)


def couple_fields(current, eps_down, eps_up):
    diverge = current[:, :, 1]
    vortic = current[:, :, 2]
    to_div = eps_down * shift_prev(vortic) + eps_up * shift_next(vortic)
    to_vort = eps_down * shift_prev(diverge) + eps_up * shift_next(diverge)
    return jnp.stack([jnp.zeros_like(to_div), to_div, to_vort], axis=2)


def forward_table(lon_count, wave_count):
    lon_index = jnp.arange(lon_count, dtype=jnp.int32)[:, None]
    wave_index = jnp.arange(wave_count, dtype=jnp.int32)[None, :]
    angles = (lon_index * wave_index % lon_count).astype(jnp.float32) * (2.0 * math.pi / lon_count)
    norm_scale = 1.0 / math.sqrt(lon_count)
    return jnp.concatenate([jnp.cos(angles) * norm_scale, -jnp.sin(angles) * norm_scale], axis=1)


def backward_table(lon_count, wave_count):
    wave_index = jnp.arange(wave_count, dtype=jnp.int32)[:, None]
    lon_index = jnp.arange(lon_count, dtype=jnp.int32)[None, :]
    angles = (lon_index * wave_index % lon_count).astype(jnp.float32) * (2.0 * math.pi / lon_count)
    doubled = jnp.where(wave_index == 0, 1.0, 2.0) / math.sqrt(lon_count)
    return jnp.concatenate([jnp.cos(angles) * doubled, -jnp.sin(angles) * doubled], axis=0)


def split_product(values, table):
    table_high = table.astype(jnp.bfloat16)
    table_low = (table - table_high.astype(jnp.float32)).astype(jnp.bfloat16)
    high_part = jnp.dot(values, table_high, preferred_element_type=jnp.float32)
    low_part = jnp.dot(values, table_low, preferred_element_type=jnp.float32)
    return high_part + low_part


def route_in(outgoing):
    return lax.all_to_all(outgoing, ("pole", "lat"), split_axis=0, concat_axis=0, tiled=True)


def route_out(outgoing):
    return lax.all_to_all(outgoing, ("pole", "lat"), split_axis=0, concat_axis=0, tiled=True)


def on_device(fields, cycle_weights, legendre, inverses, pole_coeffs, pair_order):
    mode_count, field_count, cycle_count, lon_count = fields.shape
    lat_count, per_dev, column_span = legendre.shape
    wave_count = column_span - 1
    pair_count = pair_order.shape[0]
    pole_count = inverses.shape[0]
    devices = lax.axis_size(("pole", "lat"))
    owner_index = lax.axis_index(("pole", "lat"))
    channels = mode_count * field_count
    flattened = fields.reshape(channels * cycle_count, lon_count)
    spectrum = split_product(flattened, forward_table(lon_count, wave_count))
    spectrum = spectrum.reshape(channels, cycle_count, 2, wave_count)
    weighted = (spectrum * cycle_weights[None, :, None, None]).astype(jnp.bfloat16)
    lower_half = weighted[..., :pair_count]
    upper_half = jnp.flip(weighted[..., pair_count:], axis=-1)
    halves = jnp.stack([lower_half, upper_half], axis=2)
    slotted = jnp.take(halves, pair_order, axis=4).reshape(
        channels, cycle_count, 2, 2, devices, per_dev
    )
    outgoing = jnp.transpose(slotted, (4, 1, 0, 2, 3, 5)).reshape(
        devices, cycle_count, channels * 4 * per_dev
    )
    incoming = route_in(outgoing)
    columns = incoming.reshape(lat_count, channels, 2, 2, per_dev)
    my_pairs = lax.dynamic_slice_in_dim(pair_order, owner_index * per_dev, per_dev)
    in_first, eps_down, eps_up = coupling_weights(my_pairs, wave_count, column_span)
    spec_a = jnp.einsum(
        "lcrj,ljk->crjk", columns[:, :, 0], legendre, preferred_element_type=jnp.float32
    )
    spec_b = jnp.einsum(
        "lcrj,ljk->crjk", columns[:, :, 1], legendre, preferred_element_type=jnp.float32
    )
    spectral = jnp.where(in_first, spec_a, spec_b).reshape(
        mode_count, field_count, 2, per_dev, column_span
    )
    inv_real = inverses[:, :, :, 0]
    inv_imag = inverses[:, :, :, 1]

    def apply_blocks(part_real, part_imag):
        first_term = jnp.einsum("pmjick,pmcjk->pmijk", inv_real, part_real, precision=PRECISE)
        second_term = jnp.einsum("pmjick,pmcjk->pmijk", inv_imag, part_imag, precision=PRECISE)
        third_term = jnp.einsum("pmjick,pmcjk->pmijk", inv_real, part_imag, precision=PRECISE)
        fourth_term = jnp.einsum("pmjick,pmcjk->pmijk", inv_imag, part_real, precision=PRECISE)
        return (first_term - second_term, third_term + fourth_term)

    rhs_real = jnp.broadcast_to(spectral[:, :, 0][None], (pole_count,) + spectral[:, :, 0].shape)
    rhs_imag = jnp.broadcast_to(spectral[:, :, 1][None], (pole_count,) + spectral[:, :, 1].shape)
    sol_real, sol_imag = apply_blocks(rhs_real, rhs_imag)
    for repeat in range(ITERS):
        sol_real, sol_imag = apply_blocks(
            rhs_real - couple_fields(sol_real, eps_down, eps_up),
            rhs_imag - couple_fields(sol_imag, eps_down, eps_up),
        )
    beta_real = pole_coeffs[:, 0].reshape(-1, 1, 1, 1, 1)
    beta_imag = pole_coeffs[:, 1].reshape(-1, 1, 1, 1, 1)
    comb_real = jnp.sum(beta_real * sol_real - beta_imag * sol_imag, axis=0)
    comb_imag = jnp.sum(beta_real * sol_imag + beta_imag * sol_real, axis=0)
    combined = (
        jnp.stack([comb_real, comb_imag], axis=2)
        .astype(jnp.bfloat16)
        .reshape(channels, 2, per_dev, column_span)
    )
    zero_value = jnp.zeros((), jnp.bfloat16)
    masked_a = jnp.where(in_first, combined, zero_value)
    masked_b = jnp.where(in_first, zero_value, combined)
    split_parts = jnp.stack([masked_a, masked_b], axis=1)
    synthesized = jnp.einsum(
        "csrjk,ljk->lcsrj", split_parts, legendre, preferred_element_type=jnp.float32
    ).astype(jnp.bfloat16)
    returning = route_out(synthesized.reshape(devices, cycle_count, channels * 4 * per_dev))
    blocks = returning.reshape(devices, cycle_count, channels, 2, 2, per_dev)
    blocks = jnp.transpose(blocks, (2, 1, 4, 3, 0, 5)).reshape(
        channels, cycle_count, 2, 2, pair_count
    )
    position = (
        jnp.zeros((pair_count,), jnp.int32)
        .at[pair_order]
        .set(jnp.arange(pair_count, dtype=jnp.int32))
    )
    by_pair = jnp.take(blocks, position, axis=4)
    coeffs = jnp.concatenate([by_pair[:, :, :, 0], jnp.flip(by_pair[:, :, :, 1], axis=-1)], axis=-1)
    flat_coeffs = coeffs.reshape(channels * cycle_count, 2 * wave_count)
    grid_out = split_product(flat_coeffs, backward_table(lon_count, wave_count))
    return grid_out.reshape(mode_count, field_count, cycle_count, lon_count)


def solution(mesh):
    return jax.shard_map(
        on_device,
        mesh=mesh,
        in_specs=(
            P(None, None, ("pole", "lat"), None),
            P(("pole", "lat")),
            P(None, ("pole", "lat"), None),
            P(None, None, ("pole", "lat"), None, None, None, None),
            P(),
            P(),
        ),
        out_specs=P(None, None, ("pole", "lat"), None),
        check_vma=False,
    )
```

profile of v0, /device:TPU:0, one launch (start us, length us, event | category | flops | bytes accessed | tf_op | source)
XLA Modules:
  0.0 589.0 jit_solution(13562831686603735520)
XLA Ops:
  0.0 50.5 %cosine_multiply_fusion.1 = f32[2560,1280]{1,0:T(8,128)} fusion(), kind=kLoop, calls=%fused_computation.29 | loop fusion | flops 32768000 | bytes 13107200 | tf_op jit(solution)/shard_map/mul | solution.py:56
  50.5 50.9 %negate_multiply_fusion.1 = f32[2560,1280]{1,0:T(8,128)} fusion(), kind=kLoop, calls=%fused_computation.28 | loop fusion | flops 36044800 | bytes 13107200 | tf_op jit(solution)/shard_map/mul | solution.py:56
  102.3 11.8 %fusion.8 = f32[2560,240]{0,1:T(8,128)} fusion(bf16[240,2560]{1,0:T(8,128)(2,1)S(1)} %reshape.271, f32[2560,1280]{1,0:T(8,128)} %negate_multiply_fusion.1, f32[2560,1280]{1,0:T(8,128)} %cosine_multiply_fusion.1), kind=kOutput, calls=%fused_computation.17 | convolution fusion | flops 3171942400 | bytes 29900800 | tf_op jit(solution)/shard_map/dot_general | solution.py:70
  114.2 12.8 %fusion.27 = f32[240,2560]{1,0:T(8,128)} fusion(f32[2560,240]{0,1:T(8,128)} %fusion.8, bf16[240,2560]{1,0:T(8,128)(2,1)S(1)} %reshape.271, f32[2560,1280]{1,0:T(8,128)} %negate_multiply_fusion.1, f32[2560,1280]{1,0:T(8,128)} %cosine_multiply_fusion.1), kind=kOutput, calls=%fused_computation.65 | convolution fusion | flops 3179110400 | bytes 32358400 | tf_op jit(solution)/shard_map/dot_general | solution.py:71
  141.6 34.5 %gather_fusion = bf16[640,24,10,2,2]{1,4,3,2,0:T(2,128)(2,1)} fusion(bf16[24,10,2,2,640]{0,3,4,2,1:T(2,128)(2,1)} %copy.164, s32[1024]{0:T(1024)S(1)} %pad_clamp_fusion.1), kind=kCustom, calls=%fused_computation.clone | custom fusion | bytes 2460160 | tf_op jit(solution)/shard_map/jit(_take)/gather | solution.py:99
  176.1 10.3 %broadcast_select_fusion.1 = bf16[640,24,10,2,2]{1,4,3,2,0:T(2,128)(2,1)} fusion(bf16[640,24,10,2,2]{1,4,3,2,0:T(2,128)(2,1)} %gather_fusion, pred[640]{0:T(1024)(128)(4,1)S(1)} %compare_and_fusion.1), kind=kLoop, calls=%fused_computation.36 | loop fusion | flops 614400 | bytes 2458240 | tf_op jit(solution)/shard_map/jit(_take)/select_n | solution.py:99
  186.3 14.0 %copy.166 = bf16[128,10,24,2,2,5]{0,5,4,3,2,1:T(8,128)(2,1)S(1)} copy(bf16[128,10,24,2,2,5]{2,4,3,1,5,0:T(2,128)(2,1)} %bitcast.245) | data formatting | bytes 2457600 | tf_op jit(solution)/shard_map/transpose | solution.py:102
  204.0 11.2 %all-to-all-start = ((bf16[128,10,480]{2,1,0:T(8,128)(2,1)}), bf16[128,10,480]{2,1,0:T(8,128)(2,1)S(1)}, u32[]{:S(2)}, u32[]{:S(2)}) async-start(bf16[128,10,480]{2,1,0:T(8,128)(2,1)} %copy.167), calls=%async_computation | async-start | bytes 4194304 | tf_op jit(solution)/shard_map/all_to_all | solution.py:76
  216.9 11.5 %fusion.89 = (f32[2,8,5,1,3,3,1281]{6,3,5,4,2,1,0:T(1,128)}, f32[2,8,5,1,3,3,1281]{6,3,5,4,2,1,0:T(1,128)}) fusion(f32[2,8,5,2,3,3,1281]{6,3,5,4,2,1,0:T(2,128)} %param.11), kind=kLoop, calls=%fused_computation.189 | loop fusion | bytes 14757120 | tf_op jit(solution)/shard_map/slice | solution.py:119
  228.4 16.5 %all-to-all-done = bf16[128,10,480]{2,1,0:T(8,128)(2,1)S(1)} async-done(((bf16[128,10,480]{2,1,0:T(8,128)(2,1)}), bf16[128,10,480]{2,1,0:T(8,128)(2,1)S(1)}, u32[]{:S(2)}, u32[]{:S(2)}) %all-to-all-start) | async-done | bytes 1228832 | tf_op jit(solution)/shard_map/all_to_all | solution.py:76
  244.9 13.3 %copy.168 = bf16[128,10,480]{1,0,2:T(8,128)(2,1)} copy(bf16[128,10,480]{2,1,0:T(8,128)(2,1)S(1)} %all-to-all-done) | data formatting | bytes 2457600 | tf_op jit(solution)/shard_map/all_to_all | solution.py:76
  258.2 24.6 %reshape.275 = bf16[1280,24,2,2,5]{0,4,3,2,1:T(8,128)(2,1)S(1)} reshape(bf16[128,10,480]{1,0,2:T(8,128)(2,1)} %copy.168) | data formatting | bytes 2457600 | tf_op jit(solution)/shard_map/reshape | solution.py:106
  284.3 11.1 %fusion.4 = f32[5,24,2,1281]{3,1,2,0:T(8,128)S(1)} fusion(bf16[1280,5,1281]{0,2,1:T(8,128)(2,1)} %param.10, bf16[1280,24,1,2,5]{0,4,3,2,1:T(8,128)(2,1)} %get-tuple-element.43), kind=kOutput, calls=%fused_computation.13 | convolution fusion | flops 787046400 | bytes 18240960 | tf_op jit(solution)/shard_map/lcrj,ljk->crjk/dot_general | solution.py:112
  295.3 11.1 %fusion.37 = f32[24,2,5,1281]{3,0,1,2:T(8,128)S(1)} fusion(f32[5,24,2,1281]{3,1,2,0:T(8,128)S(1)} %fusion.4, bf16[1280,5,1281]{0,2,1:T(8,128)(2,1)} %param.10, pred[5,1281]{1,0:T(8,128)(4,1)S(1)} %iota_compare_fusion, bf16[1280,24,1,2,5]{0,4,3,2,1:T(8,128)(2,1)} %get-tuple-element.42), kind=kOutput, calls=%fused_computation.69 | convolution fusion | flops 787353856 | bytes 19477124 | tf_op jit(solution)/shard_map/lcrj,ljk->crjk/dot_general | solution.py:109
  346.4 36.5 %reshape.277 = bf16[128,10,480]{1,0,2:T(8,128)(2,1)} reshape(bf16[1280,24,2,2,5]{0,4,3,2,1:T(8,128)(2,1)S(1)} %copy.186) | data formatting | bytes 2457600 | tf_op jit(solution)/shard_map/reshape | solution.py:152
  382.8 18.0 %copy.187 = bf16[128,10,480]{2,1,0:T(8,128)(2,1)} copy(bf16[128,10,480]{1,0,2:T(8,128)(2,1)} %reshape.277) | data formatting | bytes 2457600 | tf_op jit(solution)/shard_map/reshape | solution.py:152
  405.8 55.9 %cosine_multiply_fusion = (f32[1280,2560]{1,0:T(8,128)}, f32[1280,2560]{1,0:T(8,128)}) fusion(f32[1280]{0:T(1024)S(1)} %copy-done.3), kind=kLoop, calls=%fused_computation.24 | loop fusion | flops 39321600 | bytes 26219520 | tf_op jit(solution)/shard_map/mul | solution.py:64
  468.3 10.0 %copy.189 = bf16[24,10,2,2,128,5]{0,3,5,4,2,1:T(2,128)(2,1)} copy(bf16[24,10,2,2,128,5]{4,5,2,3,0,1:T(8,128)(2,1)S(1)} %bitcast.251) | data formatting | bytes 2457600 | tf_op jit(solution)/shard_map/transpose | solution.py:154
  478.3 34.3 %gather_fusion.1 = bf16[640,24,10,2,2]{1,4,3,2,0:T(2,128)(2,1)} fusion(bf16[24,10,2,2,640]{0,3,4,2,1:T(2,128)(2,1)} %bitcast.250, s32[1024]{0:T(1024)S(1)} %pad_clamp_fusion), kind=kCustom, calls=%fused_computation.1.clone | custom fusion | bytes 2460160 | tf_op jit(solution)/shard_map/jit(_take)/gather | solution.py:162
  521.6 11.6 %fusion.90 = (bf16[24,10,2,1,640]{0,3,2,1,4:T(2,128)(2,1)}, bf16[24,10,2,1,640]{0,3,2,1,4:T(2,128)(2,1)}) fusion(bf16[24,10,2,2,640]{0,3,2,1,4:T(2,128)(2,1)S(1)} %fusion.24), kind=kLoop, calls=%fused_computation.190 | loop fusion | bytes 2457600 | tf_op jit(solution)/shard_map/slice | solution.py:163
  533.2 11.5 %copy.191 = bf16[24,10,2,1,640]{4,0,3,2,1:T(8,128)(2,1)S(1)} copy(bf16[24,10,2,1,640]{0,3,2,1,4:T(2,128)(2,1)} %get-tuple-element.29) | data formatting | bytes 1228800 | tf_op jit(solution)/shard_map/slice | solution.py:163
  545.5 11.5 %copy.190 = bf16[24,10,2,1,640]{4,0,3,2,1:T(8,128)(2,1)S(1)} copy(bf16[24,10,2,1,640]{0,3,2,1,4:T(2,128)(2,1)} %get-tuple-element.28) | data formatting | bytes 1228800 | tf_op jit(solution)/shard_map/slice | solution.py:163
  558.2 11.9 %fusion.10 = f32[240,2560]{1,0:T(8,128)} fusion(bf16[240,2560]{1,0:T(8,128)(2,1)S(1)} %bitcast.261, f32[1280,2560]{1,0:T(8,128)} %get-tuple-element.89, f32[1280,2560]{1,0:T(8,128)} %get-tuple-element.88), kind=kOutput, calls=%fused_computation.18 | convolution fusion | flops 3171942400 | bytes 29900800 | tf_op jit(solution)/shard_map/dot_general | solution.py:70
  570.1 11.3 %fusion.25 = f32[240,2560]{1,0:T(8,128)S(1)} fusion(f32[240,2560]{1,0:T(8,128)} %fusion.10, bf16[240,2560]{1,0:T(8,128)(2,1)S(1)} %bitcast.262, f32[1280,2560]{1,0:T(8,128)} %get-tuple-element.89, f32[1280,2560]{1,0:T(8,128)} %get-tuple-element.88), kind=kOutput, calls=%fused_computation.63 | convolution fusion | flops 3179110400 | bytes 32358400 | tf_op jit(solution)/shard_map/dot_general | solution.py:71
  (123 shorter events, 91.7 us)
Async XLA Ops:
  50.5 50.9 %copy-start.4 = (s32[640]{0:T(1024)S(1)}, s32[640]{0:T(1024)}, u32[]{:S(2)}) copy-start(s32[640]{0:T(1024)} %param.13) | copy-start | bytes 7684
  50.5 50.9 %copy-start.2 = (bf16[8,3,10,2560]{3,0,2,1:T(8,128)(2,1)S(1)}, bf16[8,3,10,2560]{3,0,2,1:T(8,128)(2,1)}, u32[]{:S(2)}) copy-start(bf16[8,3,10,2560]{3,0,2,1:T(8,128)(2,1)} %param.8) | copy-start | bytes 3686404
  127.0 3.2 copy-start.8
  204.0 12.0 %copy-start.5 = (f32[2,2]{1,0:T(2,128)S(1)}, f32[2,2]{1,0:T(2,128)}, u32[]{:S(2)}) copy-start(f32[2,2]{1,0:T(2,128)} %param.12) | copy-start | bytes 52
  204.0 40.9 %all-to-all-start = ((bf16[128,10,480]{2,1,0:T(8,128)(2,1)}), bf16[128,10,480]{2,1,0:T(8,128)(2,1)S(1)}, u32[]{:S(2)}, u32[]{:S(2)}) async-start(bf16[128,10,480]{2,1,0:T(8,128)(2,1)} %copy.167), calls=%async_computation | async-start | bytes 4194304 | tf_op jit(solution)/shard_map/all_to_all | solution.py:76
  308.8 2.1 copy-start.1
  309.1 3.2 copy-start
  333.7 1.5 copy-start.6
  333.7 1.5 copy-start.7
  400.8 5.0 copy-start.3
  400.8 65.0 %all-to-all-start.1 = ((bf16[128,10,480]{2,1,0:T(8,128)(2,1)}), bf16[128,10,480]{2,1,0:T(8,128)(2,1)S(1)}, u32[]{:S(2)}, u32[]{:S(2)}) async-start(bf16[128,10,480]{2,1,0:T(8,128)(2,1)} %copy.187), calls=%async_computation.1 | async-start | bytes 4194304 | tf_op jit(solution)/shard_map/all_to_all | solution.py:80
where the time goes:
time: 599 us; the launch traced here: 589 us
  local copies, waits for them, and re-layouts  280 us (47%)
  other arithmetic  197 us (33%)
  matrix products  78.7 us (13%)
  waiting for transfers between devices  16.5 us (3%)
  starting transfers between devices  16.1 us (3%)
    mul x1, other arithmetic, backward_table(): jnp.cos(angles) * doubled  55.9 us
    reshape x2, local copies, waits for them, and re-layouts, on_device(): synthesized.reshape(devices, cycle_count, channels * 4 * per_dev)  54.5 us
    mul x1, other arithmetic, forward_table(): -jnp.sin(angles) * norm_scale  50.9 us
    mul x1, other arithmetic, forward_table(): jnp.cos(angles) * norm_scale  50.5 us
    gather x1, local copies, waits for them, and re-layouts, on_device(): jnp.take(halves, pair_order, axis=4)  34.5 us
    gather x1, local copies, waits for them, and re-layouts, on_device(): by_pair = jnp.take(blocks, position, axis=4)  34.3 us
    reshape x1, local copies, waits for them, and re-layouts, on_device(): columns = incoming.reshape(lat_count, channels, 2, 2, per_dev)  24.6 us
    dot_general x2, matrix products, split_product(): low_part = jnp.dot(values, table_low, preferred_element_type=jnp.float32)  24.1 us
  transfers between devices with their start and end apart: 2, of which 1 were waited for; matrix products, arithmetic and copies ran while one was open for 12% of the time, Pallas kernels for 0%

commit v1 on v0

v1 whole, which is shorter than its diff:
```python
import functools
import math

import jax
import jax.numpy as jnp
from jax import lax
from jax.experimental import pallas as pl
from jax.experimental.pallas import tpu as pltpu
from jax.sharding import PartitionSpec as P

ITERS = 3
ROTATION = 0.4
AXES = ("pole", "lat")
F32 = jnp.float32
BF16 = jnp.bfloat16
NT = (((1,), (1,)), ((), ()))
NN = (((1,), (0,)), ((), ()))

MODES, FIELDS, CYCLES, LONS = 8, 3, 10, 2560
DEVS, SLOTS, WAVES = 128, 5, 1280
HALF = LONS // 2
NLAT = DEVS * CYCLES
COLS = WAVES + 1
WIDE = 1408
HALF_CYCLES = CYCLES // 2
ROWS = 40
LANES = 128


def sin_cos(product):
    turns = jnp.floor(product * (4.0 / LONS) + 0.5)
    angle = (product - turns * (LONS / 4.0)) * (2.0 * math.pi / LONS)
    z = angle * angle
    s = angle * (1.0 + z * (-1.0 / 6 + z * (1.0 / 120 + z * (-1.0 / 5040))))
    c = 1.0 + z * (-0.5 + z * (1.0 / 24 + z * (-1.0 / 720 + z * (1.0 / 40320))))
    quarter = turns.astype(jnp.int32) & 3
    swap = (quarter & 1) == 1
    sine = jnp.where(swap, c, s)
    cosine = jnp.where(swap, s, c)
    sine = jnp.where(quarter >= 2, -sine, sine)
    cosine = jnp.where((quarter == 1) | (quarter == 2), -cosine, cosine)
    return sine, cosine


def forward_kernel(weight_ref, wave_ref, field_ref, table_ref, send_ref, grid_scr, pack_scr):
    slot = pl.program_id(0)

    @pl.when(slot == 0)
    def _():
        for half in range(2):
            for field in range(FIELDS):
                for c in range(HALF_CYCLES):
                    cycle = half * HALF_CYCLES + c
                    weight = weight_ref[cycle]
                    row = half * LANES + (field * HALF_CYCLES + c) * MODES
                    near = field_ref[field, cycle, :, :HALF].astype(F32) * weight
                    far = field_ref[field, cycle, :, HALF:].astype(F32) * weight
                    grid_scr[0, row : row + MODES, :] = (near + far).astype(BF16)
                    grid_scr[1, row : row + MODES, :] = (near - far).astype(BF16)
            row = half * LANES + FIELDS * HALF_CYCLES * MODES
            grid_scr[:, row : (half + 1) * LANES, :] = jnp.zeros((2, MODES, HALF), BF16)

    lane = lax.broadcasted_iota(jnp.int32, (32, LANES), 1).astype(F32)
    scale = 1.0 / math.sqrt(LONS)
    for parity in range(2):
        for chunk in range(4):
            wave = wave_ref[parity, 0, chunk * 32 : (chunk + 1) * 32, :]
            step_sin, step_cos = sin_cos(wave * float(LANES))
            sine, cosine = sin_cos(wave * lane)
            sine, cosine = sine * scale, cosine * scale
            for block in range(HALF // LANES):
                at = slice(block * LANES, (block + 1) * LANES)
                table_ref[parity, chunk * 32 : (chunk + 1) * 32, at] = cosine.astype(BF16)
                table_ref[parity, LANES + chunk * 32 : LANES + (chunk + 1) * 32, at] = (-sine).astype(BF16)
                sine, cosine = (
                    sine * step_cos + cosine * step_sin,
                    cosine * step_cos - sine * step_sin,
                )
        coeffs = lax.dot_general(table_ref[parity], grid_scr[parity], NT, preferred_element_type=F32)
        for part in range(2):
            for half in range(2):
                row = ((slot * 2 + parity) * 2 + part) * 2 + half
                pack_scr[pl.ds(row, DEVS, stride=ROWS), :] = coeffs[
                    part * LANES : (part + 1) * LANES, half * LANES : (half + 1) * LANES
                ]

    @pl.when(slot == SLOTS - 1)
    def _():
        send_ref[...] = pack_scr[...].astype(BF16)


def shift_prev(v):
    return pltpu.roll(v, 1, axis=1)


def shift_next(v):
    return pltpu.roll(v, WIDE - 1, axis=1)


def coupling_weights(pair):
    offset = lax.broadcasted_iota(jnp.int32, (MODES, WIDE), 1)
    in_first = offset < WAVES - pair
    order_int = jnp.where(in_first, pair, WAVES - 1 - pair)
    degree = jnp.where(in_first, pair + offset, offset - 1)
    order_m = order_int.astype(F32)
    lower_n = degree.astype(F32)
    upper_n = lower_n + 1.0
    down_ratio = jnp.maximum(lower_n * lower_n - order_m * order_m, 0.0) / jnp.maximum(
        4.0 * lower_n * lower_n - 1.0, 1.0
    )
    up_ratio = jnp.maximum(upper_n * upper_n - order_m * order_m, 0.0) / (
        4.0 * upper_n * upper_n - 1.0
    )
    real = offset < COLS
    eps_down = jnp.where((degree > order_int) & real, ROTATION * jnp.sqrt(down_ratio), 0.0)
    eps_up = jnp.where((degree + 1 < WAVES) & real, ROTATION * jnp.sqrt(up_ratio), 0.0)
    return in_first, eps_down, eps_up


def middle_kernel(
    owner_ref, pair_ref, pole_ref, recv_ref, order_ref, leg_ref, inv_ref, send_ref,
    pack_scr, cycle_scr, column_scr,
):
    slot = pl.program_id(0)

    @pl.when(slot == 0)
    def _():
        pack_scr[...] = recv_ref[...].astype(F32)
        for group in range(2 * SLOTS):
            turned = [
                jnp.transpose(pack_scr[pl.ds(group * 4 + row, DEVS, stride=ROWS), :])
                for row in range(4)
            ]
            for half in range(2):
                for c in range(HALF_CYCLES):
                    pieces = [
                        turned[part * 2 + half][
                            (field * HALF_CYCLES + c) * MODES : (field * HALF_CYCLES + c + 1) * MODES
                        ]
                        for part in range(2)
                        for field in range(FIELDS)
                    ]
                    at = (half * HALF_CYCLES + c) * LANES
                    cycle_scr[group * 48 : (group + 1) * 48, at : at + LANES] = jnp.concatenate(
                        pieces, axis=0
                    ).astype(BF16)
        column_scr[...] = lax.dot_general(
            cycle_scr[...], order_ref[...], NN, preferred_element_type=F32
        ).astype(BF16)

    pair = pair_ref[owner_ref[0] * SLOTS + slot]
    is_even = (pair & 1) == 0
    in_first, eps_down, eps_up = coupling_weights(pair)
    in_even = in_first == is_even
    rows = pl.ds(pl.multiple_of(slot * 96, 96), 96)
    column = column_scr[rows, :]
    spec = lax.dot_general(column, leg_ref[0, :WAVES, :], NT, preferred_element_type=F32)
    last = leg_ref[0, WAVES:COLS, :].astype(F32)
    spec_last = jnp.sum(column.astype(F32) * last, axis=1, keepdims=True)
    first_lane = lax.broadcasted_iota(jnp.int32, (96, LANES), 1) == 0
    spec = jnp.concatenate([spec, jnp.where(first_lane, spec_last, 0.0)], axis=1)
    rhs = [
        jnp.where(in_even, spec[g * MODES : (g + 1) * MODES], spec[48 + g * MODES : 48 + (g + 1) * MODES])
        for g in range(6)
    ]
    rhs = [(rhs[f], rhs[3 + f]) for f in range(FIELDS)]

    def couple(cur_real, cur_imag):
        return (
            eps_down * shift_prev(cur_real) + eps_up * shift_next(cur_real),
            eps_down * shift_prev(cur_imag) + eps_up * shift_next(cur_imag),
        )

    def apply(pole, row, terms):
        real, imag = None, None
        for c, (re, im) in terms:
            inv_re = inv_ref[0, pole, 0, row, c]
            inv_im = inv_ref[0, pole, 1, row, c]
            add_re = inv_re * re - inv_im * im
            add_im = inv_re * im + inv_im * re
            real = add_re if real is None else real + add_re
            imag = add_im if imag is None else imag + add_im
        return real, imag

    combined = [[None, None] for _ in range(FIELDS)]
    for pole in range(2):
        base = [apply(pole, f, list(enumerate(rhs))) for f in range(FIELDS)]
        div, vort = base[1], base[2]
        for step in range(ITERS):
            to_div, to_vort = couple(*vort), couple(*div)
            fields = range(FIELDS) if step == ITERS - 1 else (1, 2)
            solution = {}
            for f in fields:
                re, im = apply(pole, f, [(1, to_div), (2, to_vort)])
                solution[f] = (base[f][0] - re, base[f][1] - im)
            div, vort = solution[1], solution[2]
        beta_re = pole_ref[pole, 0]
        beta_im = pole_ref[pole, 1]
        for f in range(FIELDS):
            re, im = solution[f]
            add_re = beta_re * re - beta_im * im
            add_im = beta_re * im + beta_im * re
            combined[f][0] = add_re if pole == 0 else combined[f][0] + add_re
            combined[f][1] = add_im if pole == 0 else combined[f][1] + add_im

    groups = [combined[f][part] for part in range(2) for f in range(FIELDS)]
    even = jnp.concatenate([jnp.where(in_even, g, 0.0) for g in groups], axis=0)
    odd = jnp.concatenate([jnp.where(in_even, 0.0, g) for g in groups], axis=0)
    both = jnp.concatenate([even, odd], axis=0).astype(BF16)
    synth = lax.dot_general(both[:, :WAVES], leg_ref[0, :WAVES, :], NN, preferred_element_type=F32)
    synth = synth + both[:, WAVES : WAVES + 1].astype(F32) * last
    row_at = lax.broadcasted_iota(jnp.int32, (96, HALF), 0)
    synth = jnp.where((row_at < 48) & (pair == 0), synth, synth * 2.0)
    column_scr[rows, :] = synth.astype(BF16)

    @pl.when(slot == SLOTS - 1)
    def _():
        for group in range(2 * SLOTS):
            ordered = lax.dot_general(
                column_scr[group * 48 : (group + 1) * 48, :], order_ref[...], NT,
                preferred_element_type=F32,
            )
            for part in range(2):
                for half in range(2):
                    pieces = []
                    for field in range(FIELDS):
                        for c in range(HALF_CYCLES):
                            at = (half * HALF_CYCLES + c) * LANES
                            row = part * 24 + field * MODES
                            pieces.append(ordered[row : row + MODES, at : at + LANES])
                    pieces.append(jnp.zeros((MODES, LANES), F32))
                    turned = jnp.transpose(jnp.concatenate(pieces, axis=0))
                    pack_scr[pl.ds(group * 4 + part * 2 + half, DEVS, stride=ROWS), :] = turned
        send_ref[...] = pack_scr[...].astype(BF16)


def backward_kernel(recv_ref, table_ref, out_ref, pack_scr, wave_scr):
    step = pl.program_id(0)
    width = table_ref.shape[-1]

    @pl.when(step == 0)
    def _():
        pack_scr[...] = recv_ref[...].astype(F32)
        for slot in range(SLOTS):
            for parity in range(2):
                for part in range(2):
                    for half in range(2):
                        row = ((slot * 2 + parity) * 2 + part) * 2 + half
                        turned = jnp.transpose(pack_scr[pl.ds(row, DEVS, stride=ROWS), :])
                        at = (slot * 2 + part) * LANES
                        wave_scr[parity, half * LANES : (half + 1) * LANES, at : at + LANES] = turned.astype(BF16)

    even = lax.dot_general(wave_scr[0], table_ref[0], NN, preferred_element_type=F32)
    odd = lax.dot_general(wave_scr[1], table_ref[1], NN, preferred_element_type=F32)
    near = even + odd
    far = even - odd
    at = pl.multiple_of(step * width, width)
    for half in range(2):
        for field in range(FIELDS):
            for c in range(HALF_CYCLES):
                row = half * LANES + (field * HALF_CYCLES + c) * MODES
                cycle = half * HALF_CYCLES + c
                out_ref[field, cycle, :, pl.ds(at, width)] = near[row : row + MODES]
                out_ref[field, cycle, :, pl.ds(HALF + at, width)] = far[row : row + MODES]


def whole(shape):
    return pl.BlockSpec(shape, lambda i: (0,) * len(shape))


def on_device(fields, cycle_weights, legendre, inverses, pole_coeffs, pair_order):
    owner = lax.axis_index(AXES).astype(jnp.int32).reshape(1)
    smem = pl.BlockSpec(memory_space=pltpu.SMEM)
    grid_fields = jnp.transpose(fields, (1, 2, 0, 3))

    pairs = pair_order.reshape(DEVS, SLOTS).T
    is_even = (pairs & 1) == 0
    waves = jnp.stack([jnp.where(is_even, pairs, WAVES - 1 - pairs), jnp.where(is_even, WAVES - 1 - pairs, pairs)])
    waves = jnp.broadcast_to(waves.astype(F32)[..., None], (2, SLOTS, DEVS, LANES))

    table, outgoing = pl.pallas_call(
        forward_kernel,
        grid=(SLOTS,),
        in_specs=[
            smem,
            pl.BlockSpec((2, 1, DEVS, LANES), lambda i: (0, i, 0, 0)),
            whole((FIELDS, CYCLES, MODES, LONS)),
        ],
        out_specs=[
            pl.BlockSpec((2, 2 * DEVS, HALF), lambda i: (0, i, 0)),
            whole((DEVS * ROWS, LANES)),
        ],
        out_shape=[
            jax.ShapeDtypeStruct((2, HALF, HALF), BF16),
            jax.ShapeDtypeStruct((DEVS * ROWS, LANES), BF16),
        ],
        scratch_shapes=[
            pltpu.VMEM((2, 256, HALF), BF16),
            pltpu.VMEM((DEVS * ROWS, LANES), F32),
        ],
        name="forward",
    )(cycle_weights, waves, grid_fields)

    incoming = lax.all_to_all(
        outgoing.reshape(DEVS, ROWS, LANES), AXES, split_axis=0, concat_axis=0, tiled=True
    ).reshape(DEVS * ROWS, LANES)

    leg = jnp.transpose(legendre, (1, 2, 0))
    inv = jnp.transpose(inverses, (2, 0, 3, 4, 5, 1, 6))
    inv = jnp.pad(inv, ((0, 0),) * 6 + ((0, WIDE - COLS),))
    position = jnp.arange(NLAT, dtype=jnp.int32)
    natural = (position % DEVS) * CYCLES + position // DEVS
    order = (natural[:, None] == position[None, :]).astype(BF16)

    returning = pl.pallas_call(
        middle_kernel,
        grid=(SLOTS,),
        in_specs=[
            smem,
            smem,
            smem,
            whole((DEVS * ROWS, LANES)),
            whole((NLAT, NLAT)),
            pl.BlockSpec((1, COLS, NLAT), lambda i: (i, 0, 0)),
            pl.BlockSpec((1, 2, 2, 3, 3, MODES, WIDE), lambda i: (i, 0, 0, 0, 0, 0, 0)),
        ],
        out_specs=whole((DEVS * ROWS, LANES)),
        out_shape=jax.ShapeDtypeStruct((DEVS * ROWS, LANES), BF16),
        scratch_shapes=[
            pltpu.VMEM((DEVS * ROWS, LANES), F32),
            pltpu.VMEM((480, NLAT), BF16),
            pltpu.VMEM((480, NLAT), BF16),
        ],
        name="middle",
    )(owner, pair_order, pole_coeffs, incoming, order, leg, inv)

    back = lax.all_to_all(
        returning.reshape(DEVS, ROWS, LANES), AXES, split_axis=0, concat_axis=0, tiled=True
    ).reshape(DEVS * ROWS, LANES)

    width = 256
    result = pl.pallas_call(
        backward_kernel,
        grid=(HALF // width,),
        in_specs=[
            whole((DEVS * ROWS, LANES)),
            pl.BlockSpec((2, HALF, width), lambda i: (0, 0, i)),
        ],
        out_specs=whole((FIELDS, CYCLES, MODES, LONS)),
        out_shape=jax.ShapeDtypeStruct((FIELDS, CYCLES, MODES, LONS), F32),
        scratch_shapes=[
            pltpu.VMEM((DEVS * ROWS, LANES), F32),
            pltpu.VMEM((2, 256, HALF), BF16),
        ],
        name="backward",
    )(back, table)
    return jnp.transpose(result, (2, 0, 1, 3))


def solution(mesh):
    return jax.shard_map(
        on_device,
        mesh=mesh,
        in_specs=(
            P(None, None, AXES, None),
            P(AXES),
            P(None, AXES, None),
            P(None, None, AXES, None, None, None, None),
            P(),
            P(),
        ),
        out_specs=P(None, None, AXES, None),
        check_vma=False,
    )
```

time: 599 us -> 110 us (0.18); the launches traced: 589 us -> 109 us
  local copies, waits for them, and re-layouts: 280 us -> 17.1 us
  other arithmetic: 197 us -> 2.46 us
  matrix products: 78.7 us -> 0 us
  Pallas kernels: 0 us -> 45.9 us
  blocking collectives: 0 us -> 27.3 us
  waiting for transfers between devices: 16.5 us -> 5.19 us
    mul x3 -> x0, other arithmetic: 157 us -> none  [the longest x1 55.9 us: backward_table(): jnp.cos(angles) * doubled]
    reshape x10 -> x1, local copies, waits for them, and re-layouts: 94.3 us -> 0.88 us  [on_device(): pairs = pair_order.reshape(DEVS, SLOTS).T]
    dot_general x7 -> x0, matrix products: 78.7 us -> none  [the longest x2 24.1 us: split_product(): low_part = jnp.dot(values, table_low, preferred_element_type=jnp.float32)]
    gather x2 -> x0, local copies, waits for them, and re-layouts: 68.7 us -> none  [the longest x1 34.5 us: on_device(): jnp.take(halves, pair_order, axis=4)]
    slice x19 -> x0, local copies, waits for them, and re-layouts: 52.2 us -> none  [the longest x2 23.1 us: on_device(): by_pair[:, :, :, 0]]
    pallas_call x0 -> x3, Pallas kernels: none -> 45.9 us  [the longest x1 29.1 us: on_device(): pl.pallas_call(middle_kernel, grid=(SLOTS,), in_specs=[smem, smem, smem,...]
    all_to_all x0 -> x1, blocking collectives: none -> 27.3 us  [on_device(): lax.all_to_all(returning.reshape(DEVS, ROWS, LANES), AXES, split_axis=0,...]
    transpose x2 -> x0, local copies, waits for them, and re-layouts: 24 us -> none  [the longest x1 14 us: on_device(): jnp.transpose(slotted, (4, 1, 0, 2, 3, 5))]
  transfers between devices with their start and end apart: 2 -> 1, of which waited for: 1 -> 1; matrix products, arithmetic and copies ran while one was open for 12% -> 15% of each run, Pallas kernels for 0% -> 0%
where the time goes in v1:
time: 110 us; the launch traced here: 109 us
  Pallas kernels  45.9 us (42%)
  blocking collectives  27.3 us (25%)
  local copies, waits for them, and re-layouts  17.1 us (16%)
  starting transfers between devices  11.4 us (10%)
  waiting for transfers between devices  5.19 us (5%)
  other arithmetic  2.46 us (2%)
    pallas_call x1, Pallas kernels, on_device(): pl.pallas_call(middle_kernel, grid=(SLOTS,), in_specs=[smem, smem, smem,...  29.1 us
    all_to_all x1, blocking collectives, on_device(): lax.all_to_all(returning.reshape(DEVS, ROWS, LANES), AXES, split_axis=0,...  27.3 us
    all_to_all x1, starting transfers between devices, on_device(): lax.all_to_all(outgoing.reshape(DEVS, ROWS, LANES), AXES, split_axis=0, c...  11.4 us
    pallas_call x1, Pallas kernels, on_device(): pl.pallas_call(forward_kernel, grid=(SLOTS,), in_specs=[smem, pl.BlockSpe...  8.73 us
    pallas_call x1, Pallas kernels, on_device(): pl.pallas_call(backward_kernel, grid=(HALF // width,), in_specs=[whole((D...  8.08 us
    unnamed x3, local copies, waits for them, and re-layouts  8.05 us
    pad x1, local copies, waits for them, and re-layouts, on_device(): inv = jnp.pad(inv, ((0, 0),) * 6 + ((0, WIDE - COLS),))  6.95 us
    all_to_all x1, waiting for transfers between devices, on_device(): lax.all_to_all(outgoing.reshape(DEVS, ROWS, LANES), AXES, split_axis=0, c...  5.19 us
  transfers between devices with their start and end apart: 1, of which 1 were waited for; matrix products, arithmetic and copies ran while one was open for 15% of the time, Pallas kernels for 0%

profile of v1, /device:TPU:0, one launch (start us, length us, event | category | flops | bytes accessed | tf_op | source)
XLA Modules:
  0.0 109.4 jit_solution(11671257805855125802)
XLA Ops:
  0.0 0.9 reshape.58
  0.9 0.1 copy.10
  1.0 0.1 copy.11
  1.1 1.1 broadcast_in_dim.2.wave_ref
  2.2 8.7 %forward.1 = (bf16[2,1280,1280]{2,1,0:T(8,128)(2,1)}, bf16[5120,128]{1,0:T(8,128)(2,1)}) custom-call(f32[10]{0:T(128)} %weight_ref.1, f32[2,5,128,128]{3,2,1,0:T(8,128)} %broadcast_in_dim.2.wave_ref, bf16[3,10,8,2560]{3,2,1,0:T(8,128)(2,1)} %bitcast.31), custom_call_target="tpu_custom_call" | custom-call | tf_op jit(solution)/shard_map/forward/pallas_call | solution.py:281
  10.9 11.4 %all-to-all-start = ((bf16[128,40,128]{2,1,0:T(8,128)(2,1)}), bf16[128,40,128]{2,1,0:T(8,128)(2,1)S(1)}, u32[]{:S(2)}, u32[]{:S(2)}) async-start(bf16[128,40,128]{2,1,0:T(8,128)(2,1)} %bitcast.30), calls=%async_computation | async-start | bytes 2621440 | tf_op jit(solution)/shard_map/all_to_all | solution.py:304
  22.3 7.0 %copy.15 = f32[2,8,5,2,3,3,1281]{6,1,5,4,3,0,2:T(8,128)} copy(f32[2,8,5,2,3,3,1281]{6,3,5,4,2,1,0:T(2,128)} %param.9) | data formatting | bytes 14757120 | tf_op args[3]
  29.3 7.0 %pad.4.inv_ref = f32[5,2,2,3,3,8,1408]{6,5,4,3,2,1,0:T(8,128)} pad(f32[5,2,2,3,3,8,1281]{6,5,4,3,2,1,0:T(8,128)} %bitcast.25, f32[]{:T(128)} %constant.50.clone.1), padding=0_0x0_0x0_0x0_0x0_0x0_0x0_127 | pad | bytes 15488644 | tf_op jit(solution)/shard_map/jit(_pad)/pad | solution.py:310
  36.2 2.4 %fusion.order_ref = bf16[1280,1280]{1,0:T(8,128)(2,1)} fusion(s32[1280]{0:T(1024)S(1)} %fusion.10), kind=kLoop, calls=%fused_computation.2 | loop fusion | flops 3276800 | bytes 3281920 | tf_op jit(solution)/shard_map/convert_element_type | solution.py:313
  38.6 5.2 %all-to-all-done = bf16[128,40,128]{2,1,0:T(8,128)(2,1)S(1)} async-done(((bf16[128,40,128]{2,1,0:T(8,128)(2,1)}), bf16[128,40,128]{2,1,0:T(8,128)(2,1)S(1)}, u32[]{:S(2)}, u32[]{:S(2)}) %all-to-all-start) | async-done | bytes 1310752 | tf_op jit(solution)/shard_map/all_to_all | solution.py:304
  43.8 0.0 copy-start
  43.8 1.1 copy-done
  44.9 29.1 %middle.1 = bf16[5120,128]{1,0:T(8,128)(2,1)} custom-call(s32[1]{0:T(128)} %bitcast.owner_ref, s32[640]{0:T(1024)} %pair_ref.1, f32[2,2]{1,0:T(2,128)} %pole_ref.1, bf16[5120,128]{1,0:T(8,128)(2,1)} %bitcast.27, bf16[1280,1280]{1,0:T(8,128)(2,1)} %fusion.order_ref, bf16[5,1281,1280]{2,1,0:T(8,128)(2,1)} %bitcast.26, f32[5,2,2,3,3,8,1408]{6,5,4,3,2,1,0:T(8,128)} %pad.4.inv_ref), custom_call_target="tpu_custom_call" | custom-call | tf_op jit(solution)/shard_map/middle/pallas_call | solution.py:315
  74.0 27.3 %all_to_all.10 = bf16[128,40,128]{2,1,0:T(8,128)(2,1)} all-to-all(bf16[128,40,128]{2,1,0:T(8,128)(2,1)} %bitcast.28), channel_id=1, replica_groups=mesh['pole'=8,'lat'=16] {'pole','lat'}, dimensions={0} | all-to-all | bytes 2621440 | tf_op jit(solution)/shard_map/all_to_all | solution.py:337
  101.3 8.1 %backward.1 = f32[3,10,8,2560]{3,2,1,0:T(8,128)} custom-call(bf16[5120,128]{1,0:T(8,128)(2,1)} %bitcast.29, bf16[2,1280,1280]{2,1,0:T(8,128)(2,1)} %get-tuple-element.8.table_ref), custom_call_target="tpu_custom_call" | custom-call | tf_op jit(solution)/shard_map/backward/pallas_call | solution.py:342
  (4 shorter events, 0.1 us)
Async XLA Ops:
  10.9 32.9 %all-to-all-start = ((bf16[128,40,128]{2,1,0:T(8,128)(2,1)}), bf16[128,40,128]{2,1,0:T(8,128)(2,1)S(1)}, u32[]{:S(2)}, u32[]{:S(2)}) async-start(bf16[128,40,128]{2,1,0:T(8,128)(2,1)} %bitcast.30), calls=%async_computation | async-start | bytes 2621440 | tf_op jit(solution)/shard_map/all_to_all | solution.py:304
  43.8 1.1 copy-start

commit v2 on v1

v2 whole, which is shorter than its diff:
```python
import functools
import math

import jax
import jax.numpy as jnp
from jax import lax
from jax.experimental import pallas as pl
from jax.experimental.pallas import tpu as pltpu
from jax.sharding import PartitionSpec as P

ITERS = 3
ROTATION = 0.4
AXES = ("pole", "lat")
F32 = jnp.float32
BF16 = jnp.bfloat16
NT = (((1,), (1,)), ((), ()))
NN = (((1,), (0,)), ((), ()))

MODES, FIELDS, CYCLES, LONS = 8, 3, 10, 2560
DEVS, SLOTS, WAVES = 128, 5, 1280
HALF = LONS // 2
NLAT = DEVS * CYCLES
COLS = WAVES + 1
WIDE = 1408
HALF_CYCLES = CYCLES // 2
ROWS = 40
LANES = 128
SUB = 8
GROUP = 24


def sin_cos(product):
    turns = jnp.floor(product * (4.0 / LONS) + 0.5)
    angle = (product - turns * (LONS / 4.0)) * (2.0 * math.pi / LONS)
    z = angle * angle
    s = angle * (1.0 + z * (-1.0 / 6 + z * (1.0 / 120 + z * (-1.0 / 5040))))
    c = 1.0 + z * (-0.5 + z * (1.0 / 24 + z * (-1.0 / 720 + z * (1.0 / 40320))))
    quarter = turns.astype(jnp.int32) & 3
    swap = (quarter & 1) == 1
    sine = jnp.where(swap, c, s)
    cosine = jnp.where(swap, s, c)
    sine = jnp.where(quarter >= 2, -sine, sine)
    cosine = jnp.where((quarter == 1) | (quarter == 2), -cosine, cosine)
    return sine, cosine


def forward_kernel(weight_ref, pair_ref, field_ref, table_ref, send_ref, grid_scr, pack_scr):
    slot = pl.program_id(0)

    @pl.when(slot == 0)
    def _():
        for half in range(2):
            for c in range(HALF_CYCLES):
                cycle = half * HALF_CYCLES + c
                weight = weight_ref[cycle]
                for field in range(FIELDS):
                    row = half * LANES + (c * FIELDS + field) * MODES
                    near = field_ref[field, cycle, :, :HALF].astype(F32) * weight
                    far = field_ref[field, cycle, :, HALF:].astype(F32) * weight
                    grid_scr[0, row : row + MODES, :] = (near + far).astype(BF16)
                    grid_scr[1, row : row + MODES, :] = (near - far).astype(BF16)
            row = half * LANES + FIELDS * HALF_CYCLES * MODES
            grid_scr[:, row : (half + 1) * LANES, :] = jnp.zeros((2, MODES, HALF), BF16)

    place = lax.broadcasted_iota(jnp.int32, (DEVS, LANES), 0) * SLOTS + slot
    source = jnp.zeros((DEVS, LANES), jnp.int32)
    for row in range(SLOTS):
        source = jnp.where(place >> 7 == row, pair_ref[row : row + 1, :], source)
    pair = jnp.take_along_axis(source, place & (LANES - 1), axis=1)
    is_even = (pair & 1) == 0
    waves = (jnp.where(is_even, pair, WAVES - 1 - pair), jnp.where(is_even, WAVES - 1 - pair, pair))

    lane = lax.broadcasted_iota(jnp.int32, (32, LANES), 1).astype(F32)
    scale = 1.0 / math.sqrt(LONS)
    for parity in range(2):
        for chunk in range(4):
            wave = waves[parity][chunk * 32 : (chunk + 1) * 32, :].astype(F32)
            step_sin, step_cos = sin_cos(wave * float(LANES))
            sine, cosine = sin_cos(wave * lane)
            sine, cosine = sine * scale, cosine * scale
            for block in range(HALF // LANES):
                at = slice(block * LANES, (block + 1) * LANES)
                table_ref[parity, chunk * 32 : (chunk + 1) * 32, at] = cosine.astype(BF16)
                table_ref[parity, LANES + chunk * 32 : LANES + (chunk + 1) * 32, at] = (-sine).astype(BF16)
                sine, cosine = (
                    sine * step_cos + cosine * step_sin,
                    cosine * step_cos - sine * step_sin,
                )
        coeffs = lax.dot_general(table_ref[parity], grid_scr[parity], NT, preferred_element_type=F32)
        for part in range(2):
            x = parity * 2 + part
            for half in range(2):
                piece = coeffs[part * LANES : (part + 1) * LANES, half * LANES : (half + 1) * LANES]
                if x:
                    piece = pltpu.roll(piece, GROUP * x, axis=1)
                pack_scr[pl.ds(x * 2 + half, DEVS, stride=SUB), :] = piece
    send_ref[...] = pack_scr[...].reshape(DEVS, SUB, LANES).astype(BF16)


def shift_prev(v):
    return pltpu.roll(v, 1, axis=1)


def shift_next(v):
    return pltpu.roll(v, WIDE - 1, axis=1)


def coupling_weights(pair):
    offset = lax.broadcasted_iota(jnp.int32, (MODES, WIDE), 1)
    in_first = offset < WAVES - pair
    order_int = jnp.where(in_first, pair, WAVES - 1 - pair)
    degree = jnp.where(in_first, pair + offset, offset - 1)
    order_m = order_int.astype(F32)
    lower_n = degree.astype(F32)
    upper_n = lower_n + 1.0
    down_ratio = jnp.maximum(lower_n * lower_n - order_m * order_m, 0.0) / jnp.maximum(
        4.0 * lower_n * lower_n - 1.0, 1.0
    )
    up_ratio = jnp.maximum(upper_n * upper_n - order_m * order_m, 0.0) / (
        4.0 * upper_n * upper_n - 1.0
    )
    real = offset < COLS
    eps_down = jnp.where((degree > order_int) & real, ROTATION * jnp.sqrt(down_ratio), 0.0)
    eps_up = jnp.where((degree + 1 < WAVES) & real, ROTATION * jnp.sqrt(up_ratio), 0.0)
    return in_first, eps_down, eps_up


def lane_group(position):
    lane = lax.broadcasted_iota(jnp.int32, (DEVS, LANES), 1)
    lane = lane - (GROUP * position) % LANES
    lane = jnp.where(lane < 0, lane + LANES, lane)
    return lane < GROUP


def middle_kernel(
    owner_ref, pair_ref, pole_ref, recv_ref, leg_ref, inv_ref, send_ref,
    pack_scr, cycle_scr, spec_scr, base,
):
    slot = base + pl.program_id(0)

    pack_scr[...] = recv_ref[...].astype(F32).reshape(DEVS * SUB, LANES)
    for half in range(2):
        rows = [pack_scr[pl.ds(x * 2 + half, DEVS, stride=SUB), :] for x in range(4)]
        for c in range(HALF_CYCLES):
            merged = rows[3]
            for x in range(3):
                merged = jnp.where(lane_group(c + x), rows[x], merged)
            if c:
                merged = pltpu.roll(merged, LANES - GROUP * c, axis=1)
            cycle_scr[pl.ds(half * HALF_CYCLES + c, DEVS, stride=CYCLES), :] = merged
    spec_scr[:COLS, :] = lax.dot_general(
        leg_ref[0], cycle_scr[...].astype(BF16), NN, preferred_element_type=F32
    )
    spec_scr[COLS:, :] = jnp.zeros((WIDE - COLS, LANES), F32)
    spec = jnp.concatenate(
        [jnp.transpose(spec_scr[t * LANES : (t + 1) * LANES, :])[:96] for t in range(WIDE // LANES)], axis=1
    )

    pair = pair_ref[owner_ref[0] * SLOTS + slot]
    is_even = (pair & 1) == 0
    in_first, eps_down, eps_up = coupling_weights(pair)
    in_even = in_first == is_even
    rhs = [
        jnp.where(in_even, spec[g * MODES : (g + 1) * MODES], spec[48 + g * MODES : 48 + (g + 1) * MODES])
        for g in range(6)
    ]
    rhs = [(rhs[f], rhs[3 + f]) for f in range(FIELDS)]

    def block(pole, part, row, c):
        values = inv_ref[0, pole, part, row, c]
        pad = jnp.zeros((MODES, WIDE - COLS), F32)
        return jnp.concatenate([values, pad], axis=1)

    def couple(cur_real, cur_imag):
        return (
            eps_down * shift_prev(cur_real) + eps_up * shift_next(cur_real),
            eps_down * shift_prev(cur_imag) + eps_up * shift_next(cur_imag),
        )

    def apply(pole, row, terms):
        real, imag = None, None
        for c, (re, im) in terms:
            inv_re = block(pole, 0, row, c)
            inv_im = block(pole, 1, row, c)
            add_re = inv_re * re - inv_im * im
            add_im = inv_re * im + inv_im * re
            real = add_re if real is None else real + add_re
            imag = add_im if imag is None else imag + add_im
        return real, imag

    combined = [[None, None] for _ in range(FIELDS)]
    for pole in range(2):
        base = [apply(pole, f, list(enumerate(rhs))) for f in range(FIELDS)]
        div, vort = base[1], base[2]
        for step in range(ITERS):
            to_div, to_vort = couple(*vort), couple(*div)
            fields = range(FIELDS) if step == ITERS - 1 else (1, 2)
            solution = {}
            for f in fields:
                re, im = apply(pole, f, [(1, to_div), (2, to_vort)])
                solution[f] = (base[f][0] - re, base[f][1] - im)
            div, vort = solution[1], solution[2]
        beta_re = pole_ref[pole, 0]
        beta_im = pole_ref[pole, 1]
        for f in range(FIELDS):
            re, im = solution[f]
            add_re = beta_re * re - beta_im * im
            add_im = beta_re * im + beta_im * re
            combined[f][0] = add_re if pole == 0 else combined[f][0] + add_re
            combined[f][1] = add_im if pole == 0 else combined[f][1] + add_im

    groups = [combined[f][part] for part in range(2) for f in range(FIELDS)]
    even = jnp.concatenate([jnp.where(in_even, g, 0.0) for g in groups], axis=0)
    odd = jnp.concatenate([jnp.where(in_even, 0.0, g) for g in groups], axis=0)
    both = jnp.concatenate([even, odd], axis=0).astype(BF16)
    synth = lax.dot_general(both[:, :WAVES], leg_ref[0, :WAVES, :], NN, preferred_element_type=F32)
    synth = synth + both[:, WAVES : WAVES + 1].astype(F32) * leg_ref[0, WAVES:COLS, :].astype(F32)
    row_at = lax.broadcasted_iota(jnp.int32, (96, NLAT), 0)
    synth = jnp.where((row_at < 48) & (pair == 0), synth, synth * 2.0)
    synth = jnp.concatenate([synth, jnp.zeros((32, NLAT), F32)], axis=0)
    for t in range(NLAT // LANES):
        cycle_scr[t * LANES : (t + 1) * LANES, :] = jnp.transpose(synth[:, t * LANES : (t + 1) * LANES])
    for half in range(2):
        turned = []
        for c in range(HALF_CYCLES):
            values = cycle_scr[pl.ds(half * HALF_CYCLES + c, DEVS, stride=CYCLES), :]
            turned.append(pltpu.roll(values, GROUP * c, axis=1) if c else values)
        for x in range(4):
            merged = turned[HALF_CYCLES - 1]
            for c in range(HALF_CYCLES - 1):
                merged = jnp.where(lane_group(c + x), turned[c], merged)
            pack_scr[pl.ds(x * 2 + half, DEVS, stride=SUB), :] = merged
    send_ref[...] = pack_scr[...].reshape(DEVS, SUB, LANES).astype(BF16)


def backward_kernel(recv_ref, table_ref, out_ref, pack_scr, wave_scr):
    step = pl.program_id(0)
    width = table_ref.shape[-1]

    @pl.when(step == 0)
    def _():
        pack_scr[...] = recv_ref[...].astype(F32).reshape(DEVS * ROWS, LANES)
        for slot in range(SLOTS):
            for x in range(4):
                parity, part = x // 2, x % 2
                at = (slot * 2 + part) * LANES
                for half in range(2):
                    row = slot * SUB + x * 2 + half
                    turned = jnp.transpose(pack_scr[pl.ds(row, DEVS, stride=ROWS), :])
                    if x:
                        turned = jnp.concatenate([turned[GROUP * x :], turned[: GROUP * x]], axis=0)
                    wave_scr[parity, half * LANES : (half + 1) * LANES, at : at + LANES] = turned.astype(BF16)

    even = lax.dot_general(wave_scr[0], table_ref[0], NN, preferred_element_type=F32)
    odd = lax.dot_general(wave_scr[1], table_ref[1], NN, preferred_element_type=F32)
    near = even + odd
    far = even - odd
    at = pl.multiple_of(step * width, width)
    for half in range(2):
        for c in range(HALF_CYCLES):
            for field in range(FIELDS):
                row = half * LANES + (c * FIELDS + field) * MODES
                cycle = half * HALF_CYCLES + c
                out_ref[field, cycle, :, pl.ds(at, width)] = near[row : row + MODES]
                out_ref[field, cycle, :, pl.ds(HALF + at, width)] = far[row : row + MODES]


def whole(shape):
    return pl.BlockSpec(shape, lambda i: (0,) * len(shape))


def exchange(messages):
    return lax.all_to_all(messages, AXES, split_axis=0, concat_axis=0, tiled=True)


def on_device(fields, cycle_weights, legendre, inverses, pole_coeffs, pair_order):
    owner = lax.axis_index(AXES).astype(jnp.int32).reshape(1)
    smem = pl.BlockSpec(memory_space=pltpu.SMEM)
    grid_fields = jnp.transpose(fields, (1, 2, 0, 3))

    table, outgoing = pl.pallas_call(
        forward_kernel,
        grid=(SLOTS,),
        in_specs=[
            smem,
            whole((SLOTS, LANES)),
            whole((FIELDS, CYCLES, MODES, LONS)),
        ],
        out_specs=[
            pl.BlockSpec((2, 2 * DEVS, HALF), lambda i: (0, i, 0)),
            pl.BlockSpec((DEVS, SUB, LANES), lambda i: (0, i, 0)),
        ],
        out_shape=[
            jax.ShapeDtypeStruct((2, HALF, HALF), BF16),
            jax.ShapeDtypeStruct((DEVS, ROWS, LANES), BF16),
        ],
        scratch_shapes=[
            pltpu.VMEM((2, 256, HALF), BF16),
            pltpu.VMEM((DEVS * SUB, LANES), F32),
        ],
        name="forward",
    )(cycle_weights, pair_order.reshape(SLOTS, LANES), grid_fields)

    incoming = exchange(outgoing)

    leg = jnp.transpose(legendre, (1, 2, 0))
    inv = jnp.transpose(inverses, (2, 0, 3, 4, 5, 1, 6))

    returning = pl.pallas_call(
        functools.partial(middle_kernel, base=0),
        grid=(SLOTS,),
        in_specs=[
            smem,
            smem,
            smem,
            pl.BlockSpec((DEVS, SUB, LANES), lambda i: (0, i, 0)),
            pl.BlockSpec((1, COLS, NLAT), lambda i: (i, 0, 0)),
            pl.BlockSpec((1, 2, 2, 3, 3, MODES, COLS), lambda i: (i, 0, 0, 0, 0, 0, 0)),
        ],
        out_specs=pl.BlockSpec((DEVS, SUB, LANES), lambda i: (0, i, 0)),
        out_shape=jax.ShapeDtypeStruct((DEVS, ROWS, LANES), BF16),
        scratch_shapes=[
            pltpu.VMEM((DEVS * SUB, LANES), F32),
            pltpu.VMEM((NLAT, LANES), F32),
            pltpu.VMEM((WIDE, LANES), F32),
        ],
        name="middle",
    )(owner, pair_order, pole_coeffs, incoming, leg, inv)

    back = exchange(returning)

    width = 256
    result = pl.pallas_call(
        backward_kernel,
        grid=(HALF // width,),
        in_specs=[
            whole((DEVS, ROWS, LANES)),
            pl.BlockSpec((2, HALF, width), lambda i: (0, 0, i)),
        ],
        out_specs=whole((FIELDS, CYCLES, MODES, LONS)),
        out_shape=jax.ShapeDtypeStruct((FIELDS, CYCLES, MODES, LONS), F32),
        scratch_shapes=[
            pltpu.VMEM((DEVS * ROWS, LANES), F32),
            pltpu.VMEM((2, 256, HALF), BF16),
        ],
        name="backward",
    )(back, table)
    return jnp.transpose(result, (2, 0, 1, 3))


def solution(mesh):
    return jax.shard_map(
        on_device,
        mesh=mesh,
        in_specs=(
            P(None, None, AXES, None),
            P(AXES),
            P(None, AXES, None),
            P(None, None, AXES, None, None, None, None),
            P(),
            P(),
        ),
        out_specs=P(None, None, AXES, None),
        check_vma=False,
    )
```

time: 110 us -> 100 us (0.909)
  waiting for transfers between devices: 5.19 us -> 14.8 us
  local copies, waits for them, and re-layouts: 17.1 us -> 7.99 us
  Pallas kernels: 45.9 us -> 38.5 us
  other arithmetic: 2.46 us -> 0 us
    all_to_all x1, waiting for transfers between devices: 5.19 us -> 14.8 us  [exchange(): lax.all_to_all(messages, AXES, split_axis=0, concat_axis=0, tiled=True)]
    pallas_call x2, Pallas kernels: 37.9 us -> 30.4 us  [the longest x1 21.8 us: on_device(): pl.pallas_call(functools.partial(middle_kernel, base=0), grid=(SLOTS,), i...]
    pad x1 -> x0, local copies, waits for them, and re-layouts: 6.95 us -> none  [on_device(): inv = jnp.pad(inv, ((0, 0),) * 6 + ((0, WIDE - COLS),))]
    convert_element_type x2 -> x0, other arithmetic: 2.44 us -> none  [the longest x1 2.41 us: on_device(): order = (natural[:, None] == position[None, :]).astype(BF16)]
  transfers between devices with their start and end apart: 1 -> 1, of which waited for: 1 -> 1; matrix products, arithmetic and copies ran while one was open for 15% -> 7% of each run, Pallas kernels for 0% -> 0%
where the time goes in v2:
time: 100 us; the launch traced here: 99.8 us
  Pallas kernels  38.5 us (38%)
  blocking collectives  27.3 us (27%)
  waiting for transfers between devices  14.8 us (15%)
  starting transfers between devices  11.2 us (11%)
  local copies, waits for them, and re-layouts  7.99 us (8%)
    all_to_all x1, blocking collectives, exchange(): lax.all_to_all(messages, AXES, split_axis=0, concat_axis=0, tiled=True)  27.3 us
    pallas_call x1, Pallas kernels, on_device(): pl.pallas_call(functools.partial(middle_kernel, base=0), grid=(SLOTS,), i...  21.8 us
    all_to_all x1, waiting for transfers between devices, exchange(): lax.all_to_all(messages, AXES, split_axis=0, concat_axis=0, tiled=True)  14.8 us
    all_to_all x1, starting transfers between devices, exchange(): lax.all_to_all(messages, AXES, split_axis=0, concat_axis=0, tiled=True)  11.2 us
    pallas_call x1, Pallas kernels, on_device(): pl.pallas_call(forward_kernel, grid=(SLOTS,), in_specs=[smem, whole((SLOT...  8.67 us
    pallas_call x1, Pallas kernels, on_device(): pl.pallas_call(backward_kernel, grid=(HALF // width,), in_specs=[whole((D...  8.08 us
    unnamed x3, local copies, waits for them, and re-layouts  7.99 us
  transfers between devices with their start and end apart: 1, of which 1 were waited for; matrix products, arithmetic and copies ran while one was open for 7% of the time, Pallas kernels for 0%

profile of v2, /device:TPU:0, one launch (start us, length us, event | category | flops | bytes accessed | tf_op | source)
XLA Modules:
  0.0 99.8 jit_solution(4150186659975131320)
XLA Ops:
  0.0 8.7 %forward.1 = (bf16[2,1280,1280]{2,1,0:T(8,128)(2,1)}, bf16[128,40,128]{2,1,0:T(8,128)(2,1)}) custom-call(f32[10]{0:T(128)} %weight_ref.1, s32[5,128]{1,0:T(8,128)} %bitcast.11, bf16[3,10,8,2560]{3,2,1,0:T(8,128)(2,1)} %bitcast.10), custom_call_target="tpu_custom_call" | custom-call | tf_op jit(solution)/shard_map/forward/pallas_call | solution.py:281
  8.7 11.2 %all-to-all-start = ((bf16[128,40,128]{2,1,0:T(8,128)(2,1)}), bf16[128,40,128]{2,1,0:T(8,128)(2,1)S(1)}, u32[]{:S(2)}, u32[]{:S(2)}) async-start(bf16[128,40,128]{2,1,0:T(8,128)(2,1)} %get-tuple-element.7), calls=%async_computation | async-start | bytes 2621440 | tf_op jit(solution)/shard_map/all_to_all | solution.py:273
  19.9 6.9 %copy.9 = f32[2,8,5,2,3,3,1281]{6,1,5,4,3,0,2:T(8,128)} copy(f32[2,8,5,2,3,3,1281]{6,3,5,4,2,1,0:T(2,128)} %param.9) | data formatting | bytes 14757120 | tf_op args[3]
  26.8 14.8 %all-to-all-done.recv_ref = bf16[128,40,128]{2,1,0:T(8,128)(2,1)S(1)} async-done(((bf16[128,40,128]{2,1,0:T(8,128)(2,1)}), bf16[128,40,128]{2,1,0:T(8,128)(2,1)S(1)}, u32[]{:S(2)}, u32[]{:S(2)}) %all-to-all-start) | async-done | bytes 1310752 | tf_op jit(solution)/shard_map/all_to_all | solution.py:273
  41.6 0.0 copy-start
  41.6 1.1 %copy-done = bf16[128,40,128]{2,1,0:T(8,128)(2,1)} copy-done((bf16[128,40,128]{2,1,0:T(8,128)(2,1)}, bf16[128,40,128]{2,1,0:T(8,128)(2,1)S(1)}, u32[]{:S(2)}) %copy-start) | copy-done | bytes 1310744
  42.7 21.8 %middle.1 = bf16[128,40,128]{2,1,0:T(8,128)(2,1)} custom-call(s32[1]{0:T(128)} %bitcast.owner_ref, s32[640]{0:T(1024)} %pair_ref.1, f32[2,2]{1,0:T(2,128)} %pole_ref.1, bf16[128,40,128]{2,1,0:T(8,128)(2,1)} %copy-done, bf16[5,1281,1280]{2,1,0:T(8,128)(2,1)} %bitcast.9, f32[5,2,2,3,3,8,1281]{6,5,4,3,2,1,0:T(8,128)} %bitcast.8), custom_call_target="tpu_custom_call" | custom-call | tf_op jit(solution)/shard_map/middle/pallas_call | solution.py:309
  64.4 27.3 %all_to_all.10.recv_ref = bf16[128,40,128]{2,1,0:T(8,128)(2,1)} all-to-all(bf16[128,40,128]{2,1,0:T(8,128)(2,1)} %middle.1), channel_id=1, replica_groups=mesh['pole'=8,'lat'=16] {'pole','lat'}, dimensions={0} | all-to-all | bytes 2621440 | tf_op jit(solution)/shard_map/all_to_all | solution.py:273
  91.7 8.1 %backward.1 = f32[3,10,8,2560]{3,2,1,0:T(8,128)} custom-call(bf16[128,40,128]{2,1,0:T(8,128)(2,1)} %all_to_all.10.recv_ref, bf16[2,1280,1280]{2,1,0:T(8,128)(2,1)} %get-tuple-element.8.table_ref), custom_call_target="tpu_custom_call" | custom-call | tf_op jit(solution)/shard_map/backward/pallas_call | solution.py:333
Async XLA Ops:
  8.7 32.9 %all-to-all-start = ((bf16[128,40,128]{2,1,0:T(8,128)(2,1)}), bf16[128,40,128]{2,1,0:T(8,128)(2,1)S(1)}, u32[]{:S(2)}, u32[]{:S(2)}) async-start(bf16[128,40,128]{2,1,0:T(8,128)(2,1)} %get-tuple-element.7), calls=%async_computation | async-start | bytes 2621440 | tf_op jit(solution)/shard_map/all_to_all | solution.py:273
  41.6 1.1 %copy-start = (bf16[128,40,128]{2,1,0:T(8,128)(2,1)}, bf16[128,40,128]{2,1,0:T(8,128)(2,1)S(1)}, u32[]{:S(2)}) copy-start(bf16[128,40,128]{2,1,0:T(8,128)(2,1)S(1)} %all-to-all-done.recv_ref) | copy-start | bytes 3932164

commit v3 on v2

--- a/solution.py
+++ b/solution.py
@@ -1,4 +1,3 @@
-import functools
 import math
 
 import jax
@@ -134,9 +133,9 @@
 
 def middle_kernel(
     owner_ref, pair_ref, pole_ref, recv_ref, leg_ref, inv_ref, send_ref,
-    pack_scr, cycle_scr, spec_scr, base,
+    pack_scr, cycle_scr,
 ):
-    slot = base + pl.program_id(0)
+    slot = pl.program_id(0)
 
     pack_scr[...] = recv_ref[...].astype(F32).reshape(DEVS * SUB, LANES)
     for half in range(2):
@@ -148,13 +147,14 @@
             if c:
                 merged = pltpu.roll(merged, LANES - GROUP * c, axis=1)
             cycle_scr[pl.ds(half * HALF_CYCLES + c, DEVS, stride=CYCLES), :] = merged
-    spec_scr[:COLS, :] = lax.dot_general(
-        leg_ref[0], cycle_scr[...].astype(BF16), NN, preferred_element_type=F32
+    column = jnp.concatenate(
+        [jnp.transpose(cycle_scr[t * LANES : (t + 1) * LANES, :])[:96] for t in range(NLAT // LANES)], axis=1
     )
-    spec_scr[COLS:, :] = jnp.zeros((WIDE - COLS, LANES), F32)
-    spec = jnp.concatenate(
-        [jnp.transpose(spec_scr[t * LANES : (t + 1) * LANES, :])[:96] for t in range(WIDE // LANES)], axis=1
-    )
+    last = leg_ref[0, WAVES:COLS, :].astype(F32)
+    spec_last = jnp.sum(column * last, axis=1, keepdims=True)
+    spec = lax.dot_general(column.astype(BF16), leg_ref[0, :WAVES, :], NT, preferred_element_type=F32)
+    first_lane = lax.broadcasted_iota(jnp.int32, (96, LANES), 1) == 0
+    spec = jnp.concatenate([spec, jnp.where(first_lane, spec_last, 0.0)], axis=1)
 
     pair = pair_ref[owner_ref[0] * SLOTS + slot]
     is_even = (pair & 1) == 0
@@ -166,11 +166,6 @@
     ]
     rhs = [(rhs[f], rhs[3 + f]) for f in range(FIELDS)]
 
-    def block(pole, part, row, c):
-        values = inv_ref[0, pole, part, row, c]
-        pad = jnp.zeros((MODES, WIDE - COLS), F32)
-        return jnp.concatenate([values, pad], axis=1)
-
     def couple(cur_real, cur_imag):
         return (
             eps_down * shift_prev(cur_real) + eps_up * shift_next(cur_real),
@@ -180,8 +175,8 @@
     def apply(pole, row, terms):
         real, imag = None, None
         for c, (re, im) in terms:
-            inv_re = block(pole, 0, row, c)
-            inv_im = block(pole, 1, row, c)
+            inv_re = inv_ref[0, pole, 0, row, c]
+            inv_im = inv_ref[0, pole, 1, row, c]
             add_re = inv_re * re - inv_im * im
             add_im = inv_re * im + inv_im * re
             real = add_re if real is None else real + add_re
@@ -214,7 +209,7 @@
     odd = jnp.concatenate([jnp.where(in_even, 0.0, g) for g in groups], axis=0)
     both = jnp.concatenate([even, odd], axis=0).astype(BF16)
     synth = lax.dot_general(both[:, :WAVES], leg_ref[0, :WAVES, :], NN, preferred_element_type=F32)
-    synth = synth + both[:, WAVES : WAVES + 1].astype(F32) * leg_ref[0, WAVES:COLS, :].astype(F32)
+    synth = synth + both[:, WAVES : WAVES + 1].astype(F32) * last
     row_at = lax.broadcasted_iota(jnp.int32, (96, NLAT), 0)
     synth = jnp.where((row_at < 48) & (pair == 0), synth, synth * 2.0)
     synth = jnp.concatenate([synth, jnp.zeros((32, NLAT), F32)], axis=0)
@@ -305,9 +300,10 @@
 
     leg = jnp.transpose(legendre, (1, 2, 0))
     inv = jnp.transpose(inverses, (2, 0, 3, 4, 5, 1, 6))
+    inv = jnp.pad(inv, ((0, 0),) * 6 + ((0, WIDE - COLS),))
 
     returning = pl.pallas_call(
-        functools.partial(middle_kernel, base=0),
+        middle_kernel,
         grid=(SLOTS,),
         in_specs=[
             smem,
@@ -315,15 +311,15 @@
             smem,
             pl.BlockSpec((DEVS, SUB, LANES), lambda i: (0, i, 0)),
             pl.BlockSpec((1, COLS, NLAT), lambda i: (i, 0, 0)),
-            pl.BlockSpec((1, 2, 2, 3, 3, MODES, COLS), lambda i: (i, 0, 0, 0, 0, 0, 0)),
+            pl.BlockSpec((1, 2, 2, 3, 3, MODES, WIDE), lambda i: (i, 0, 0, 0, 0, 0, 0)),
         ],
         out_specs=pl.BlockSpec((DEVS, SUB, LANES), lambda i: (0, i, 0)),
         out_shape=jax.ShapeDtypeStruct((DEVS, ROWS, LANES), BF16),
         scratch_shapes=[
             pltpu.VMEM((DEVS * SUB, LANES), F32),
             pltpu.VMEM((NLAT, LANES), F32),
-            pltpu.VMEM((WIDE, LANES), F32),
-        ],
+        ],
+        compiler_params=pltpu.CompilerParams(vmem_limit_bytes=32 << 20),
         name="middle",
     )(owner, pair_order, pole_coeffs, incoming, leg, inv)
 

time: 100 us -> 96.9 us (0.969)
  local copies, waits for them, and re-layouts: 7.99 us -> 17.3 us
  waiting for transfers between devices: 14.8 us -> 7.77 us
  Pallas kernels: 38.5 us -> 33.9 us
    all_to_all x1, waiting for transfers between devices: 14.8 us -> 7.77 us  [exchange(): lax.all_to_all(messages, AXES, split_axis=0, concat_axis=0, tiled=True)]
    pad x0 -> x1, local copies, waits for them, and re-layouts: none -> 7.02 us  [on_device(): inv = jnp.pad(inv, ((0, 0),) * 6 + ((0, WIDE - COLS),))]
    pallas_call x1, Pallas kernels: 21.8 us -> 17.1 us  [on_device(): pl.pallas_call(middle_kernel, grid=(SLOTS,), in_specs=[smem, smem, smem,...]
    unnamed x3 -> x7, local copies, waits for them, and re-layouts: 7.99 us -> 10.3 us
  transfers between devices with their start and end apart: 1 -> 1, of which waited for: 1 -> 1; matrix products, arithmetic and copies ran while one was open for 7% -> 14% of each run, Pallas kernels for 0% -> 0%
where the time goes in v3:
time: 96.9 us; the launch traced here: 96.5 us
  Pallas kernels  33.9 us (35%)
  blocking collectives  26.4 us (27%)
  local copies, waits for them, and re-layouts  17.3 us (18%)
  starting transfers between devices  11.2 us (12%)
  waiting for transfers between devices  7.77 us (8%)
    all_to_all x1, blocking collectives, exchange(): lax.all_to_all(messages, AXES, split_axis=0, concat_axis=0, tiled=True)  26.4 us
    pallas_call x1, Pallas kernels, on_device(): pl.pallas_call(middle_kernel, grid=(SLOTS,), in_specs=[smem, smem, smem,...  17.1 us
    all_to_all x1, starting transfers between devices, exchange(): lax.all_to_all(messages, AXES, split_axis=0, concat_axis=0, tiled=True)  11.2 us
    unnamed x7, local copies, waits for them, and re-layouts  10.3 us
    pallas_call x1, Pallas kernels, on_device(): pl.pallas_call(forward_kernel, grid=(SLOTS,), in_specs=[smem, whole((SLOT...  8.67 us
    pallas_call x1, Pallas kernels, on_device(): pl.pallas_call(backward_kernel, grid=(HALF // width,), in_specs=[whole((D...  8.08 us
    all_to_all x1, waiting for transfers between devices, exchange(): lax.all_to_all(messages, AXES, split_axis=0, concat_axis=0, tiled=True)  7.77 us
    pad x1, local copies, waits for them, and re-layouts, on_device(): inv = jnp.pad(inv, ((0, 0),) * 6 + ((0, WIDE - COLS),))  7.02 us
  transfers between devices with their start and end apart: 1, of which 1 were waited for; matrix products, arithmetic and copies ran while one was open for 14% of the time, Pallas kernels for 0%

profile of v3, /device:TPU:0, one launch (start us, length us, event | category | flops | bytes accessed | tf_op | source)
XLA Modules:
  0.0 96.5 jit_solution(10114695184635786073)
XLA Ops:
  0.0 8.7 %forward.1 = (bf16[2,1280,1280]{2,1,0:T(8,128)(2,1)}, bf16[128,40,128]{2,1,0:T(8,128)(2,1)}) custom-call(f32[10]{0:T(128)} %weight_ref.1, s32[5,128]{1,0:T(8,128)} %bitcast.8, bf16[3,10,8,2560]{3,2,1,0:T(8,128)(2,1)} %bitcast.11), custom_call_target="tpu_custom_call" | custom-call | tf_op jit(solution)/shard_map/forward/pallas_call | solution.py:276
  8.7 11.2 %all-to-all-start = ((bf16[128,40,128]{2,1,0:T(8,128)(2,1)}), bf16[128,40,128]{2,1,0:T(8,128)(2,1)S(1)}, u32[]{:S(2)}, u32[]{:S(2)}) async-start(bf16[128,40,128]{2,1,0:T(8,128)(2,1)} %get-tuple-element.7), calls=%async_computation | async-start | bytes 2621440 | tf_op jit(solution)/shard_map/all_to_all | solution.py:268
  19.9 6.9 %copy.9 = f32[2,8,5,2,3,3,1281]{6,1,5,4,3,0,2:T(8,128)} copy(f32[2,8,5,2,3,3,1281]{6,3,5,4,2,1,0:T(2,128)} %param.9) | data formatting | bytes 14757120 | tf_op args[3]
  26.8 0.0 copy-start.1
  26.8 0.0 copy-start.2
  26.8 7.0 %pad.4.inv_ref = f32[5,2,2,3,3,8,1408]{6,5,4,3,2,1,0:T(8,128)} pad(f32[5,2,2,3,3,8,1281]{6,5,4,3,2,1,0:T(8,128)} %bitcast.9, f32[]{:T(128)} %constant.13.clone.1), padding=0_0x0_0x0_0x0_0x0_0x0_0x0_127 | pad | bytes 15488644 | tf_op jit(solution)/shard_map/jit(_pad)/pad | solution.py:303
  33.8 7.8 %all-to-all-done.recv_ref = bf16[128,40,128]{2,1,0:T(8,128)(2,1)S(1)} async-done(((bf16[128,40,128]{2,1,0:T(8,128)(2,1)}), bf16[128,40,128]{2,1,0:T(8,128)(2,1)S(1)}, u32[]{:S(2)}, u32[]{:S(2)}) %all-to-all-start) | async-done | bytes 1310752 | tf_op jit(solution)/shard_map/all_to_all | solution.py:268
  41.6 0.0 copy-done.1
  41.6 0.0 copy-done.2
  41.6 0.0 copy-start
  41.6 3.3 %copy-done = f32[5,2,2,3,3,8,1408]{6,5,4,3,2,1,0:T(8,128)S(1)} copy-done((f32[5,2,2,3,3,8,1408]{6,5,4,3,2,1,0:T(8,128)S(1)}, f32[5,2,2,3,3,8,1408]{6,5,4,3,2,1,0:T(8,128)}, u32[]{:S(2)}) %copy-start) | copy-done | bytes 8110104
  44.9 17.1 %middle.1 = bf16[128,40,128]{2,1,0:T(8,128)(2,1)S(1)} custom-call(s32[1]{0:T(128)} %bitcast.owner_ref, s32[640]{0:T(1024)S(1)} %copy-done.1, f32[2,2]{1,0:T(2,128)S(1)} %copy-done.2, bf16[128,40,128]{2,1,0:T(8,128)(2,1)S(1)} %all-to-all-done.recv_ref, bf16[5,1281,1280]{2,1,0:T(8,128)(2,1)} %bitcast.10, f32[5,2,2,3,3,8,1408]{6,5,4,3,2,1,0:T(8,128)S(1)} %copy-done), custom_call_target="tpu_custom_call" | custom-call | tf_op jit(solution)/shard_map/middle/pallas_call | solution.py:305
  62.0 26.4 %all_to_all.10.recv_ref = bf16[128,40,128]{2,1,0:T(8,128)(2,1)} all-to-all(bf16[128,40,128]{2,1,0:T(8,128)(2,1)S(1)} %middle.1), channel_id=1, replica_groups=mesh['pole'=8,'lat'=16] {'pole','lat'}, dimensions={0} | all-to-all | bytes 2621440 | tf_op jit(solution)/shard_map/all_to_all | solution.py:268
  88.5 8.1 %backward.1 = f32[3,10,8,2560]{3,2,1,0:T(8,128)} custom-call(bf16[128,40,128]{2,1,0:T(8,128)(2,1)} %all_to_all.10.recv_ref, bf16[2,1280,1280]{2,1,0:T(8,128)(2,1)} %get-tuple-element.8.table_ref), custom_call_target="tpu_custom_call" | custom-call | tf_op jit(solution)/shard_map/backward/pallas_call | solution.py:329
Async XLA Ops:
  8.7 32.9 %all-to-all-start = ((bf16[128,40,128]{2,1,0:T(8,128)(2,1)}), bf16[128,40,128]{2,1,0:T(8,128)(2,1)S(1)}, u32[]{:S(2)}, u32[]{:S(2)}) async-start(bf16[128,40,128]{2,1,0:T(8,128)(2,1)} %get-tuple-element.7), calls=%async_computation | async-start | bytes 2621440 | tf_op jit(solution)/shard_map/all_to_all | solution.py:268
  26.8 14.8 %copy-start.1 = (s32[640]{0:T(1024)S(1)}, s32[640]{0:T(1024)}, u32[]{:S(2)}) copy-start(s32[640]{0:T(1024)} %pair_ref.1) | copy-start | bytes 7684
  26.8 14.8 %copy-start.2 = (f32[2,2]{1,0:T(2,128)S(1)}, f32[2,2]{1,0:T(2,128)}, u32[]{:S(2)}) copy-start(f32[2,2]{1,0:T(2,128)} %pole_ref.1) | copy-start | bytes 52
  41.6 3.3 %copy-start = (f32[5,2,2,3,3,8,1408]{6,5,4,3,2,1,0:T(8,128)S(1)}, f32[5,2,2,3,3,8,1408]{6,5,4,3,2,1,0:T(8,128)}, u32[]{:S(2)}) copy-start(f32[5,2,2,3,3,8,1408]{6,5,4,3,2,1,0:T(8,128)} %pad.4.inv_ref) | copy-start | bytes 24330244

commit v4 on v3

--- a/solution.py
+++ b/solution.py
@@ -319,7 +319,7 @@
             pltpu.VMEM((DEVS * SUB, LANES), F32),
             pltpu.VMEM((NLAT, LANES), F32),
         ],
-        compiler_params=pltpu.CompilerParams(vmem_limit_bytes=32 << 20),
+        compiler_params=pltpu.CompilerParams(vmem_limit_bytes=50 << 20),
         name="middle",
     )(owner, pair_order, pole_coeffs, incoming, leg, inv)
 
@@ -339,6 +339,7 @@
             pltpu.VMEM((DEVS * ROWS, LANES), F32),
             pltpu.VMEM((2, 256, HALF), BF16),
         ],
+        compiler_params=pltpu.CompilerParams(vmem_limit_bytes=20 << 20),
         name="backward",
     )(back, table)
     return jnp.transpose(result, (2, 0, 1, 3))

time: 96.9 us -> 90.7 us (0.936)
  local copies, waits for them, and re-layouts: 17.3 us -> 14 us
  Pallas kernels: 33.9 us -> 31.7 us
    unnamed x7 -> x9, local copies, waits for them, and re-layouts: 10.3 us -> 6.96 us
    pallas_call x1, Pallas kernels: 8.08 us -> 5.19 us  [on_device(): pl.pallas_call(backward_kernel, grid=(HALF // width,), in_specs=[whole((D...]
  transfers between devices with their start and end apart: 1 -> 1, of which waited for: 1 -> 1; matrix products, arithmetic and copies ran while one was open for 14% -> 15% of each run, Pallas kernels for 0% -> 0%
where the time goes in v4:
time: 90.7 us; the launch traced here: 90.4 us
  Pallas kernels  31.7 us (35%)
  blocking collectives  25.7 us (28%)
  local copies, waits for them, and re-layouts  14 us (15%)
  starting transfers between devices  11.2 us (12%)
  waiting for transfers between devices  7.77 us (9%)
    all_to_all x1, blocking collectives, exchange(): lax.all_to_all(messages, AXES, split_axis=0, concat_axis=0, tiled=True)  25.7 us
    pallas_call x1, Pallas kernels, on_device(): pl.pallas_call(middle_kernel, grid=(SLOTS,), in_specs=[smem, smem, smem,...  17.8 us
    all_to_all x1, starting transfers between devices, exchange(): lax.all_to_all(messages, AXES, split_axis=0, concat_axis=0, tiled=True)  11.2 us
    pallas_call x1, Pallas kernels, on_device(): pl.pallas_call(forward_kernel, grid=(SLOTS,), in_specs=[smem, whole((SLOT...  8.67 us
    all_to_all x1, waiting for transfers between devices, exchange(): lax.all_to_all(messages, AXES, split_axis=0, concat_axis=0, tiled=True)  7.77 us
    pad x1, local copies, waits for them, and re-layouts, on_device(): inv = jnp.pad(inv, ((0, 0),) * 6 + ((0, WIDE - COLS),))  7.02 us
    unnamed x9, local copies, waits for them, and re-layouts  6.96 us
    pallas_call x1, Pallas kernels, on_device(): pl.pallas_call(backward_kernel, grid=(HALF // width,), in_specs=[whole((D...  5.19 us
  transfers between devices with their start and end apart: 1, of which 1 were waited for; matrix products, arithmetic and copies ran while one was open for 15% of the time, Pallas kernels for 0%

profile of v4, /device:TPU:0, one launch (start us, length us, event | category | flops | bytes accessed | tf_op | source)
XLA Modules:
  0.0 90.4 jit_solution(6685119776480892572)
XLA Ops:
  0.0 8.7 %forward.1 = (bf16[2,1280,1280]{2,1,0:T(8,128)(2,1)}, bf16[128,40,128]{2,1,0:T(8,128)(2,1)}) custom-call(f32[10]{0:T(128)} %weight_ref.1, s32[5,128]{1,0:T(8,128)} %bitcast.10, bf16[3,10,8,2560]{3,2,1,0:T(8,128)(2,1)} %bitcast.13), custom_call_target="tpu_custom_call" | custom-call | tf_op jit(solution)/shard_map/forward/pallas_call | solution.py:276
  8.7 11.2 %all-to-all-start = ((bf16[128,40,128]{2,1,0:T(8,128)(2,1)}), bf16[128,40,128]{2,1,0:T(8,128)(2,1)S(1)}, u32[]{:S(2)}, u32[]{:S(2)}) async-start(bf16[128,40,128]{2,1,0:T(8,128)(2,1)} %get-tuple-element.7), calls=%async_computation | async-start | bytes 2621440 | tf_op jit(solution)/shard_map/all_to_all | solution.py:268
  19.9 6.9 %copy.9 = f32[2,8,5,2,3,3,1281]{6,1,5,4,3,0,2:T(8,128)} copy(f32[2,8,5,2,3,3,1281]{6,3,5,4,2,1,0:T(2,128)} %param.9) | data formatting | bytes 14757120 | tf_op args[3]
  26.8 0.0 copy-start
  26.8 0.0 copy-start.1
  26.8 7.0 %pad.4.inv_ref = f32[5,2,2,3,3,8,1408]{6,5,4,3,2,1,0:T(8,128)} pad(f32[5,2,2,3,3,8,1281]{6,5,4,3,2,1,0:T(8,128)} %bitcast.11, f32[]{:T(128)} %constant.13.clone.1), padding=0_0x0_0x0_0x0_0x0_0x0_0x0_127 | pad | bytes 15488644 | tf_op jit(solution)/shard_map/jit(_pad)/pad | solution.py:303
  33.8 7.8 %all-to-all-done.recv_ref = bf16[128,40,128]{2,1,0:T(8,128)(2,1)S(1)} async-done(((bf16[128,40,128]{2,1,0:T(8,128)(2,1)}), bf16[128,40,128]{2,1,0:T(8,128)(2,1)S(1)}, u32[]{:S(2)}, u32[]{:S(2)}) %all-to-all-start) | async-done | bytes 1310752 | tf_op jit(solution)/shard_map/all_to_all | solution.py:268
  41.6 0.0 slice-start
  41.6 0.0 copy-done
  41.6 0.0 copy-done.1
  41.6 0.0 slice-start.1
  41.6 17.8 %middle.1 = bf16[128,40,128]{2,1,0:T(8,128)(2,1)S(1)} custom-call(s32[1]{0:T(128)} %bitcast.owner_ref, s32[640]{0:T(1024)S(1)} %copy-done, f32[2,2]{1,0:T(2,128)S(1)} %copy-done.1, bf16[128,40,128]{2,1,0:T(8,128)(2,1)S(1)} %all-to-all-done.recv_ref, bf16[5,1281,1280]{2,1,0:T(8,128)(2,1)} %bitcast.12, f32[5,2,2,3,3,8,1408]{6,5,4,3,2,1,0:T(8,128)} %pad.4.inv_ref), custom_call_target="tpu_custom_call" | custom-call | tf_op jit(solution)/shard_map/middle/pallas_call | solution.py:305
  59.4 25.7 %all_to_all.10.recv_ref = bf16[128,40,128]{2,1,0:T(8,128)(2,1)S(1)} all-to-all(bf16[128,40,128]{2,1,0:T(8,128)(2,1)S(1)} %middle.1), channel_id=1, replica_groups=mesh['pole'=8,'lat'=16] {'pole','lat'}, dimensions={0} | all-to-all | bytes 2621440 | tf_op jit(solution)/shard_map/all_to_all | solution.py:268
  85.2 0.0 slice-done
  85.2 0.0 slice-done.1
  85.2 5.2 %backward.1 = f32[3,10,8,2560]{3,2,1,0:T(8,128)} custom-call(bf16[128,40,128]{2,1,0:T(8,128)(2,1)S(1)} %all_to_all.10.recv_ref, bf16[2,1280,1280]{2,1,0:T(8,128)(2,1)S(1)} %bitcast.9), custom_call_target="tpu_custom_call" | custom-call | tf_op jit(solution)/shard_map/backward/pallas_call | solution.py:329
  (1 shorter events, 0.0 us)
Async XLA Ops:
  8.7 32.9 %all-to-all-start = ((bf16[128,40,128]{2,1,0:T(8,128)(2,1)}), bf16[128,40,128]{2,1,0:T(8,128)(2,1)S(1)}, u32[]{:S(2)}, u32[]{:S(2)}) async-start(bf16[128,40,128]{2,1,0:T(8,128)(2,1)} %get-tuple-element.7), calls=%async_computation | async-start | bytes 2621440 | tf_op jit(solution)/shard_map/all_to_all | solution.py:268
  26.8 14.8 %copy-start = (s32[640]{0:T(1024)S(1)}, s32[640]{0:T(1024)}, u32[]{:S(2)}) copy-start(s32[640]{0:T(1024)} %pair_ref.1) | copy-start | bytes 7684
  26.8 14.8 %copy-start.1 = (f32[2,2]{1,0:T(2,128)S(1)}, f32[2,2]{1,0:T(2,128)}, u32[]{:S(2)}) copy-start(f32[2,2]{1,0:T(2,128)} %pole_ref.1) | copy-start | bytes 52
  41.6 43.6 %slice-start = ((s8[6553600]{0:T(1024)(128)(4,1)}), s8[4194304]{0:T(1024)(128)(4,1)S(1)}, s32[]{:S(2)}) async-start(s8[6553600]{0:T(1024)(128)(4,1)} %bitcast.8), calls=%async_computation.2 | async-start | bytes 8388608
  41.6 43.6 %slice-start.1 = ((s8[6553600]{0:T(1024)(128)(4,1)}), s8[2359296]{0:T(1024)(128)(4,1)S(1)}, s32[]{:S(2)}) async-start(s8[6553600]{0:T(1024)(128)(4,1)} %bitcast.8), calls=%async_computation.3 | async-start | bytes 4718592

commit v5 on v4

--- a/solution.py
+++ b/solution.py
@@ -61,30 +61,53 @@
             row = half * LANES + FIELDS * HALF_CYCLES * MODES
             grid_scr[:, row : (half + 1) * LANES, :] = jnp.zeros((2, MODES, HALF), BF16)
 
-    place = lax.broadcasted_iota(jnp.int32, (DEVS, LANES), 0) * SLOTS + slot
-    source = jnp.zeros((DEVS, LANES), jnp.int32)
+    place = lax.broadcasted_iota(jnp.int32, (SUB, LANES), 1) * SLOTS + slot
+    pair = jnp.zeros((SUB, LANES), jnp.int32)
     for row in range(SLOTS):
-        source = jnp.where(place >> 7 == row, pair_ref[row : row + 1, :], source)
-    pair = jnp.take_along_axis(source, place & (LANES - 1), axis=1)
+        source = jnp.broadcast_to(pair_ref[row : row + 1, :], (SUB, LANES))
+        found = jnp.take_along_axis(source, place & (LANES - 1), axis=1)
+        pair = jnp.where(place >> 7 == row, found, pair)
     is_even = (pair & 1) == 0
-    waves = (jnp.where(is_even, pair, WAVES - 1 - pair), jnp.where(is_even, WAVES - 1 - pair, pair))
-
-    lane = lax.broadcasted_iota(jnp.int32, (32, LANES), 1).astype(F32)
+    even = jnp.where(is_even, pair, WAVES - 1 - pair)
+    waves = (even, WAVES - 1 - even)
+
+    def down(row):
+        return jnp.transpose(jnp.broadcast_to(row[:1], (LANES, LANES)))
+
+    turns = [[down(v) for v in sin_cos(wave.astype(F32) * float(LANES))] for wave in waves]
+    signs = [down(jnp.where((wave & 2) == 0, 1.0, -1.0).astype(F32)) for wave in waves]
+    even = down(even.astype(F32))
+
+    lane = lax.broadcasted_iota(jnp.int32, (1, LANES), 1)
+    alternate = jnp.where((lane & 1) == 0, 1.0, -1.0)
+    to_odd_sin, to_odd_cos = (v * alternate for v in sin_cos(lane.astype(F32)))
     scale = 1.0 / math.sqrt(LONS)
+    for chunk in range(4):
+        part = slice(chunk * 32, (chunk + 1) * 32)
+        sine, cosine = sin_cos(even[part] * lane.astype(F32))
+        cosine, minus = cosine * scale, sine * -scale
+        starts = (
+            (cosine, minus),
+            (cosine * to_odd_cos + minus * to_odd_sin, cosine * to_odd_sin - minus * to_odd_cos),
+        )
+        for parity in range(2):
+            cosine, minus = starts[parity]
+            step_sin, step_cos = (v[part] for v in turns[parity])
+            sign = signs[parity][part].astype(BF16)
+            low = slice(LANES + chunk * 32, LANES + (chunk + 1) * 32)
+            for block in range(HALF // LANES // 2):
+                at = slice(block * LANES, (block + 1) * LANES)
+                later = slice(HALF // 2 + block * LANES, HALF // 2 + (block + 1) * LANES)
+                re, im = cosine.astype(BF16), minus.astype(BF16)
+                table_ref[parity, part, at] = re
+                table_ref[parity, low, at] = im
+                table_ref[parity, part, later] = im * sign if parity else re * sign
+                table_ref[parity, low, later] = -re * sign if parity else im * sign
+                cosine, minus = (
+                    cosine * step_cos + minus * step_sin,
+                    minus * step_cos - cosine * step_sin,
+                )
     for parity in range(2):
-        for chunk in range(4):
-            wave = waves[parity][chunk * 32 : (chunk + 1) * 32, :].astype(F32)
-            step_sin, step_cos = sin_cos(wave * float(LANES))
-            sine, cosine = sin_cos(wave * lane)
-            sine, cosine = sine * scale, cosine * scale
-            for block in range(HALF // LANES):
-                at = slice(block * LANES, (block + 1) * LANES)
-                table_ref[parity, chunk * 32 : (chunk + 1) * 32, at] = cosine.astype(BF16)
-                table_ref[parity, LANES + chunk * 32 : LANES + (chunk + 1) * 32, at] = (-sine).astype(BF16)
-                sine, cosine = (
-                    sine * step_cos + cosine * step_sin,
-                    cosine * step_cos - sine * step_sin,
-                )
         coeffs = lax.dot_general(table_ref[parity], grid_scr[parity], NT, preferred_element_type=F32)
         for part in range(2):
             x = parity * 2 + part
@@ -131,12 +154,7 @@
     return lane < GROUP
 
 
-def middle_kernel(
-    owner_ref, pair_ref, pole_ref, recv_ref, leg_ref, inv_ref, send_ref,
-    pack_scr, cycle_scr,
-):
-    slot = pl.program_id(0)
-
+def unpack_columns(recv_ref, pack_scr, cycle_scr):
     pack_scr[...] = recv_ref[...].astype(F32).reshape(DEVS * SUB, LANES)
     for half in range(2):
         rows = [pack_scr[pl.ds(x * 2 + half, DEVS, stride=SUB), :] for x in range(4)]
@@ -147,25 +165,20 @@
             if c:
                 merged = pltpu.roll(merged, LANES - GROUP * c, axis=1)
             cycle_scr[pl.ds(half * HALF_CYCLES + c, DEVS, stride=CYCLES), :] = merged
-    column = jnp.concatenate(
+    return jnp.concatenate(
         [jnp.transpose(cycle_scr[t * LANES : (t + 1) * LANES, :])[:96] for t in range(NLAT // LANES)], axis=1
     )
-    last = leg_ref[0, WAVES:COLS, :].astype(F32)
+
+
+def analyse(column, leg_ref):
+    last = leg_ref[WAVES:COLS, :].astype(F32)
     spec_last = jnp.sum(column * last, axis=1, keepdims=True)
-    spec = lax.dot_general(column.astype(BF16), leg_ref[0, :WAVES, :], NT, preferred_element_type=F32)
+    spec = lax.dot_general(column.astype(BF16), leg_ref[:WAVES, :], NT, preferred_element_type=F32)
     first_lane = lax.broadcasted_iota(jnp.int32, (96, LANES), 1) == 0
-    spec = jnp.concatenate([spec, jnp.where(first_lane, spec_last, 0.0)], axis=1)
-
-    pair = pair_ref[owner_ref[0] * SLOTS + slot]
-    is_even = (pair & 1) == 0
-    in_first, eps_down, eps_up = coupling_weights(pair)
-    in_even = in_first == is_even
-    rhs = [
-        jnp.where(in_even, spec[g * MODES : (g + 1) * MODES], spec[48 + g * MODES : 48 + (g + 1) * MODES])
-        for g in range(6)
-    ]
-    rhs = [(rhs[f], rhs[3 + f]) for f in range(FIELDS)]
-
+    return spec, jnp.where(first_lane, spec_last, 0.0)
+
+
+def solve(rhs, inv_ref, pole_ref, eps_down, eps_up):
     def couple(cur_real, cur_imag):
         return (
             eps_down * shift_prev(cur_real) + eps_up * shift_next(cur_real),
@@ -175,8 +188,8 @@
     def apply(pole, row, terms):
         real, imag = None, None
         for c, (re, im) in terms:
-            inv_re = inv_ref[0, pole, 0, row, c]
-            inv_im = inv_ref[0, pole, 1, row, c]
+            inv_re = inv_ref[pole, 0, row, c]
+            inv_im = inv_ref[pole, 1, row, c]
             add_re = inv_re * re - inv_im * im
             add_im = inv_re * im + inv_im * re
             real = add_re if real is None else real + add_re
@@ -203,15 +216,20 @@
             add_im = beta_re * im + beta_im * re
             combined[f][0] = add_re if pole == 0 else combined[f][0] + add_re
             combined[f][1] = add_im if pole == 0 else combined[f][1] + add_im
-
-    groups = [combined[f][part] for part in range(2) for f in range(FIELDS)]
+    return [combined[f][part] for part in range(2) for f in range(FIELDS)]
+
+
+def synthesize(groups, in_even, pair, leg_ref):
     even = jnp.concatenate([jnp.where(in_even, g, 0.0) for g in groups], axis=0)
     odd = jnp.concatenate([jnp.where(in_even, 0.0, g) for g in groups], axis=0)
     both = jnp.concatenate([even, odd], axis=0).astype(BF16)
-    synth = lax.dot_general(both[:, :WAVES], leg_ref[0, :WAVES, :], NN, preferred_element_type=F32)
-    synth = synth + both[:, WAVES : WAVES + 1].astype(F32) * last
+    synth = lax.dot_general(both[:, :WAVES], leg_ref[:WAVES, :], NN, preferred_element_type=F32)
+    synth = synth + both[:, WAVES : WAVES + 1].astype(F32) * leg_ref[WAVES:COLS, :].astype(F32)
     row_at = lax.broadcasted_iota(jnp.int32, (96, NLAT), 0)
-    synth = jnp.where((row_at < 48) & (pair == 0), synth, synth * 2.0)
+    return jnp.where((row_at < 48) & (pair == 0), synth, synth * 2.0)
+
+
+def pack_messages(synth, send_ref, pack_scr, cycle_scr):
     synth = jnp.concatenate([synth, jnp.zeros((32, NLAT), F32)], axis=0)
     for t in range(NLAT // LANES):
         cycle_scr[t * LANES : (t + 1) * LANES, :] = jnp.transpose(synth[:, t * LANES : (t + 1) * LANES])
@@ -228,6 +246,73 @@
     send_ref[...] = pack_scr[...].reshape(DEVS, SUB, LANES).astype(BF16)
 
 
+def middle_kernel(
+    owner_ref, pair_ref, pole_ref, recv_ref, leg_hbm, inv_hbm, send_ref,
+    leg_scr, inv_scr, spec_scr, pack_in, cycle_in, pack_out, cycle_out, leg_sem, inv_sem,
+):
+    step = pl.program_id(0)
+
+    def leg_copy(slot):
+        return pltpu.make_async_copy(leg_hbm.at[slot], leg_scr.at[slot], leg_sem.at[slot])
+
+    def inv_copy(slot):
+        return pltpu.make_async_copy(inv_hbm.at[slot], inv_scr.at[slot], inv_sem.at[slot])
+
+    def store_spec(spec, spec_last):
+        spec_scr[:, :WAVES] = spec
+        spec_scr[:, WAVES:] = spec_last
+
+    def right_side(slot):
+        pair = pair_ref[owner_ref[0] * SLOTS + slot]
+        in_first, eps_down, eps_up = coupling_weights(pair)
+        in_even = in_first == ((pair & 1) == 0)
+        rhs = [
+            jnp.where(in_even, spec_scr[g * MODES : (g + 1) * MODES, :], spec_scr[48 + g * MODES : 56 + g * MODES, :])
+            for g in range(6)
+        ]
+        return pair, in_even, [(rhs[f], rhs[3 + f]) for f in range(FIELDS)], eps_down, eps_up
+
+    @pl.when(step == 0)
+    def _():
+        leg_copy(0).start()
+        inv_copy(0).start()
+        leg_copy(1).start()
+        column = unpack_columns(recv_ref, pack_in, cycle_in)
+        leg_copy(0).wait()
+        inv_copy(1).start()
+        leg_copy(2).start()
+        store_spec(*analyse(column, leg_scr.at[0]))
+
+    @pl.when((step > 0) & (step < SLOTS))
+    def _():
+        inv_copy(step - 1).wait()
+        leg_copy(step).wait()
+
+        @pl.when(step + 1 < SLOTS)
+        def _():
+            inv_copy(step + 1).start()
+
+        @pl.when(step + 2 < SLOTS)
+        def _():
+            leg_copy(step + 2).start()
+
+        pair, in_even, rhs, eps_down, eps_up = right_side(step - 1)
+        column = unpack_columns(recv_ref, pack_in, cycle_in)
+        spec = analyse(column, leg_scr.at[step])
+        groups = solve(rhs, inv_scr.at[step - 1], pole_ref, eps_down, eps_up)
+        store_spec(*spec)
+        synth = synthesize(groups, in_even, pair, leg_scr.at[step - 1])
+        pack_messages(synth, send_ref, pack_out, cycle_out)
+
+    @pl.when(step == SLOTS)
+    def _():
+        inv_copy(SLOTS - 1).wait()
+        pair, in_even, rhs, eps_down, eps_up = right_side(SLOTS - 1)
+        groups = solve(rhs, inv_scr.at[SLOTS - 1], pole_ref, eps_down, eps_up)
+        synth = synthesize(groups, in_even, pair, leg_scr.at[SLOTS - 1])
+        pack_messages(synth, send_ref, pack_out, cycle_out)
+
+
 def backward_kernel(recv_ref, table_ref, out_ref, pack_scr, wave_scr):
     step = pl.program_id(0)
     width = table_ref.shape[-1]
@@ -302,22 +387,30 @@
     inv = jnp.transpose(inverses, (2, 0, 3, 4, 5, 1, 6))
     inv = jnp.pad(inv, ((0, 0),) * 6 + ((0, WIDE - COLS),))
 
+    anywhere = pl.BlockSpec(memory_space=pl.ANY)
     returning = pl.pallas_call(
         middle_kernel,
-        grid=(SLOTS,),
+        grid=(SLOTS + 1,),
         in_specs=[
             smem,
             smem,
             smem,
-            pl.BlockSpec((DEVS, SUB, LANES), lambda i: (0, i, 0)),
-            pl.BlockSpec((1, COLS, NLAT), lambda i: (i, 0, 0)),
-            pl.BlockSpec((1, 2, 2, 3, 3, MODES, WIDE), lambda i: (i, 0, 0, 0, 0, 0, 0)),
-        ],
-        out_specs=pl.BlockSpec((DEVS, SUB, LANES), lambda i: (0, i, 0)),
+            pl.BlockSpec((DEVS, SUB, LANES), lambda i: (0, jnp.minimum(i, SLOTS - 1), 0)),
+            anywhere,
+            anywhere,
+        ],
+        out_specs=pl.BlockSpec((DEVS, SUB, LANES), lambda i: (0, jnp.maximum(i - 1, 0), 0)),
         out_shape=jax.ShapeDtypeStruct((DEVS, ROWS, LANES), BF16),
         scratch_shapes=[
+            pltpu.VMEM((SLOTS, COLS, NLAT), BF16),
+            pltpu.VMEM((SLOTS, 2, 2, 3, 3, MODES, WIDE), F32),
+            pltpu.VMEM((96, WIDE), F32),
             pltpu.VMEM((DEVS * SUB, LANES), F32),
             pltpu.VMEM((NLAT, LANES), F32),
+            pltpu.VMEM((DEVS * SUB, LANES), F32),
+            pltpu.VMEM((NLAT, LANES), F32),
+            pltpu.SemaphoreType.DMA((SLOTS,)),
+            pltpu.SemaphoreType.DMA((SLOTS,)),
         ],
         compiler_params=pltpu.CompilerParams(vmem_limit_bytes=50 << 20),
         name="middle",

time: 90.7 us -> 89.7 us (0.989)
  transfers between devices with their start and end apart: 1 -> 1, of which waited for: 1 -> 1; matrix products, arithmetic and copies ran while one was open for 15% -> 16% of each run, Pallas kernels for 0% -> 0%
where the time goes in v5:
time: 89.7 us; the launch traced here: 89.4 us
  Pallas kernels  30.8 us (34%)
  blocking collectives  25.7 us (29%)
  local copies, waits for them, and re-layouts  14 us (16%)
  starting transfers between devices  11.2 us (12%)
  waiting for transfers between devices  7.77 us (9%)
    all_to_all x1, blocking collectives, exchange(): lax.all_to_all(messages, AXES, split_axis=0, concat_axis=0, tiled=True)  25.7 us
    pallas_call x1, Pallas kernels, on_device(): pl.pallas_call(middle_kernel, grid=(SLOTS + 1,), in_specs=[smem, smem, sm...  17.3 us
    all_to_all x1, starting transfers between devices, exchange(): lax.all_to_all(messages, AXES, split_axis=0, concat_axis=0, tiled=True)  11.2 us
    pallas_call x1, Pallas kernels, on_device(): pl.pallas_call(forward_kernel, grid=(SLOTS,), in_specs=[smem, whole((SLOT...  8.27 us
    all_to_all x1, waiting for transfers between devices, exchange(): lax.all_to_all(messages, AXES, split_axis=0, concat_axis=0, tiled=True)  7.77 us
    pad x1, local copies, waits for them, and re-layouts, on_device(): inv = jnp.pad(inv, ((0, 0),) * 6 + ((0, WIDE - COLS),))  7.02 us
    unnamed x9, local copies, waits for them, and re-layouts  6.96 us
    pallas_call x1, Pallas kernels, on_device(): pl.pallas_call(backward_kernel, grid=(HALF // width,), in_specs=[whole((D...  5.19 us
  transfers between devices with their start and end apart: 1, of which 1 were waited for; matrix products, arithmetic and copies ran while one was open for 16% of the time, Pallas kernels for 0%

profile of v5, /device:TPU:0, one launch (start us, length us, event | category | flops | bytes accessed | tf_op | source)
XLA Modules:
  0.0 89.4 jit_solution(12924354991737112865)
XLA Ops:
  0.0 8.3 %forward.1 = (bf16[2,1280,1280]{2,1,0:T(8,128)(2,1)}, bf16[128,40,128]{2,1,0:T(8,128)(2,1)}) custom-call(f32[10]{0:T(128)} %weight_ref.1, s32[5,128]{1,0:T(8,128)} %bitcast.10, bf16[3,10,8,2560]{3,2,1,0:T(8,128)(2,1)} %bitcast.13), custom_call_target="tpu_custom_call" | custom-call | tf_op jit(solution)/shard_map/forward/pallas_call | solution.py:361
  8.3 11.2 %all-to-all-start = ((bf16[128,40,128]{2,1,0:T(8,128)(2,1)}), bf16[128,40,128]{2,1,0:T(8,128)(2,1)S(1)}, u32[]{:S(2)}, u32[]{:S(2)}) async-start(bf16[128,40,128]{2,1,0:T(8,128)(2,1)} %get-tuple-element.7), calls=%async_computation | async-start | bytes 2621440 | tf_op jit(solution)/shard_map/all_to_all | solution.py:353
  19.5 6.9 %copy.9 = f32[2,8,5,2,3,3,1281]{6,1,5,4,3,0,2:T(8,128)} copy(f32[2,8,5,2,3,3,1281]{6,3,5,4,2,1,0:T(2,128)} %param.9) | data formatting | bytes 14757120 | tf_op args[3]
  26.4 0.0 copy-start
  26.4 0.0 copy-start.1
  26.4 7.0 %pad.4.inv_hbm = f32[5,2,2,3,3,8,1408]{6,5,4,3,2,1,0:T(8,128)} pad(f32[5,2,2,3,3,8,1281]{6,5,4,3,2,1,0:T(8,128)} %bitcast.11, f32[]{:T(128)} %constant.13.clone.1), padding=0_0x0_0x0_0x0_0x0_0x0_0x0_127 | pad | bytes 15488644 | tf_op jit(solution)/shard_map/jit(_pad)/pad | solution.py:388
  33.4 7.8 %all-to-all-done.recv_ref = bf16[128,40,128]{2,1,0:T(8,128)(2,1)S(1)} async-done(((bf16[128,40,128]{2,1,0:T(8,128)(2,1)}), bf16[128,40,128]{2,1,0:T(8,128)(2,1)S(1)}, u32[]{:S(2)}, u32[]{:S(2)}) %all-to-all-start) | async-done | bytes 1310752 | tf_op jit(solution)/shard_map/all_to_all | solution.py:353
  41.2 0.0 slice-start
  41.2 0.0 copy-done
  41.2 0.0 copy-done.1
  41.2 0.0 slice-start.1
  41.2 17.3 %middle.1 = bf16[128,40,128]{2,1,0:T(8,128)(2,1)S(1)} custom-call(s32[1]{0:T(128)} %bitcast.owner_ref, s32[640]{0:T(1024)S(1)} %copy-done, f32[2,2]{1,0:T(2,128)S(1)} %copy-done.1, bf16[128,40,128]{2,1,0:T(8,128)(2,1)S(1)} %all-to-all-done.recv_ref, bf16[5,1281,1280]{2,1,0:T(8,128)(2,1)} %bitcast.12, f32[5,2,2,3,3,8,1408]{6,5,4,3,2,1,0:T(8,128)} %pad.4.inv_hbm), custom_call_target="tpu_custom_call" | custom-call | tf_op jit(solution)/shard_map/middle/pallas_call | solution.py:391
  58.5 25.7 %all_to_all.10.recv_ref = bf16[128,40,128]{2,1,0:T(8,128)(2,1)S(1)} all-to-all(bf16[128,40,128]{2,1,0:T(8,128)(2,1)S(1)} %middle.1), channel_id=1, replica_groups=mesh['pole'=8,'lat'=16] {'pole','lat'}, dimensions={0} | all-to-all | bytes 2621440 | tf_op jit(solution)/shard_map/all_to_all | solution.py:353
  84.2 0.0 slice-done
  84.2 0.0 slice-done.1
  84.3 5.2 %backward.1 = f32[3,10,8,2560]{3,2,1,0:T(8,128)} custom-call(bf16[128,40,128]{2,1,0:T(8,128)(2,1)S(1)} %all_to_all.10.recv_ref, bf16[2,1280,1280]{2,1,0:T(8,128)(2,1)S(1)} %bitcast.9), custom_call_target="tpu_custom_call" | custom-call | tf_op jit(solution)/shard_map/backward/pallas_call | solution.py:422
  (1 shorter events, 0.0 us)
Async XLA Ops:
  8.3 32.9 %all-to-all-start = ((bf16[128,40,128]{2,1,0:T(8,128)(2,1)}), bf16[128,40,128]{2,1,0:T(8,128)(2,1)S(1)}, u32[]{:S(2)}, u32[]{:S(2)}) async-start(bf16[128,40,128]{2,1,0:T(8,128)(2,1)} %get-tuple-element.7), calls=%async_computation | async-start | bytes 2621440 | tf_op jit(solution)/shard_map/all_to_all | solution.py:353
  26.4 14.8 %copy-start = (s32[640]{0:T(1024)S(1)}, s32[640]{0:T(1024)}, u32[]{:S(2)}) copy-start(s32[640]{0:T(1024)} %pair_ref.1) | copy-start | bytes 7684
  26.4 14.8 %copy-start.1 = (f32[2,2]{1,0:T(2,128)S(1)}, f32[2,2]{1,0:T(2,128)}, u32[]{:S(2)}) copy-start(f32[2,2]{1,0:T(2,128)} %pole_ref.1) | copy-start | bytes 52
  41.2 43.1 %slice-start = ((s8[6553600]{0:T(1024)(128)(4,1)}), s8[4194304]{0:T(1024)(128)(4,1)S(1)}, s32[]{:S(2)}) async-start(s8[6553600]{0:T(1024)(128)(4,1)} %bitcast.8), calls=%async_computation.2 | async-start | bytes 8388608
  41.2 43.0 %slice-start.1 = ((s8[6553600]{0:T(1024)(128)(4,1)}), s8[2359296]{0:T(1024)(128)(4,1)S(1)}, s32[]{:S(2)}) async-start(s8[6553600]{0:T(1024)(128)(4,1)} %bitcast.8), calls=%async_computation.3 | async-start | bytes 4718592

commit v6 on v5

--- a/solution.py
+++ b/solution.py
@@ -247,13 +247,16 @@
 
 
 def middle_kernel(
-    owner_ref, pair_ref, pole_ref, recv_ref, leg_hbm, inv_hbm, send_ref,
+    owner_ref, pair_ref, pole_ref, recv_ref, leg_first, leg_hbm, inv_hbm, send_ref,
     leg_scr, inv_scr, spec_scr, pack_in, cycle_in, pack_out, cycle_out, leg_sem, inv_sem,
 ):
     step = pl.program_id(0)
 
     def leg_copy(slot):
         return pltpu.make_async_copy(leg_hbm.at[slot], leg_scr.at[slot], leg_sem.at[slot])
+
+    def first_copy():
+        return pltpu.make_async_copy(leg_first, leg_scr.at[0], leg_sem.at[0])
 
     def inv_copy(slot):
         return pltpu.make_async_copy(inv_hbm.at[slot], inv_scr.at[slot], inv_sem.at[slot])
@@ -274,11 +277,11 @@
 
     @pl.when(step == 0)
     def _():
-        leg_copy(0).start()
+        first_copy().start()
         inv_copy(0).start()
         leg_copy(1).start()
         column = unpack_columns(recv_ref, pack_in, cycle_in)
-        leg_copy(0).wait()
+        first_copy().wait()
         inv_copy(1).start()
         leg_copy(2).start()
         store_spec(*analyse(column, leg_scr.at[0]))
@@ -313,7 +316,7 @@
         pack_messages(synth, send_ref, pack_out, cycle_out)
 
 
-def backward_kernel(recv_ref, table_ref, out_ref, pack_scr, wave_scr):
+def backward_kernel(recv_ref, table_ref, out_hbm, pack_scr, wave_scr, out_scr, out_sem):
     step = pl.program_id(0)
     width = table_ref.shape[-1]
 
@@ -335,14 +338,40 @@
     odd = lax.dot_general(wave_scr[1], table_ref[1], NN, preferred_element_type=F32)
     near = even + odd
     far = even - odd
-    at = pl.multiple_of(step * width, width)
+    slot = step % 2
+
+    def leave(when):
+        at = pl.multiple_of(when * width, width)
+        return [
+            pltpu.make_async_copy(
+                out_scr.at[when % 2, side],
+                out_hbm.at[:, :, :, pl.ds(side * HALF + at, width)],
+                out_sem.at[when % 2, side],
+            )
+            for side in range(2)
+        ]
+
+    @pl.when(step >= 2)
+    def _():
+        for copy in leave(step - 2):
+            copy.wait()
+
     for half in range(2):
         for c in range(HALF_CYCLES):
             for field in range(FIELDS):
                 row = half * LANES + (c * FIELDS + field) * MODES
                 cycle = half * HALF_CYCLES + c
-                out_ref[field, cycle, :, pl.ds(at, width)] = near[row : row + MODES]
-                out_ref[field, cycle, :, pl.ds(HALF + at, width)] = far[row : row + MODES]
+                out_scr[slot, 0, field, cycle, :, :] = near[row : row + MODES]
+                out_scr[slot, 1, field, cycle, :, :] = far[row : row + MODES]
+
+    for copy in leave(step):
+        copy.start()
+
+    @pl.when(step == pl.num_programs(0) - 1)
+    def _():
+        for when in (step - 1, step):
+            for copy in leave(when):
+                copy.wait()
 
 
 def whole(shape):
@@ -396,6 +425,7 @@
             smem,
             smem,
             pl.BlockSpec((DEVS, SUB, LANES), lambda i: (0, jnp.minimum(i, SLOTS - 1), 0)),
+            anywhere,
             anywhere,
             anywhere,
         ],
@@ -412,9 +442,9 @@
             pltpu.SemaphoreType.DMA((SLOTS,)),
             pltpu.SemaphoreType.DMA((SLOTS,)),
         ],
-        compiler_params=pltpu.CompilerParams(vmem_limit_bytes=50 << 20),
+        compiler_params=pltpu.CompilerParams(vmem_limit_bytes=46 << 20),
         name="middle",
-    )(owner, pair_order, pole_coeffs, incoming, leg, inv)
+    )(owner, pair_order, pole_coeffs, incoming, leg[0], leg, inv)
 
     back = exchange(returning)
 
@@ -426,11 +456,13 @@
             whole((DEVS, ROWS, LANES)),
             pl.BlockSpec((2, HALF, width), lambda i: (0, 0, i)),
         ],
-        out_specs=whole((FIELDS, CYCLES, MODES, LONS)),
+        out_specs=anywhere,
         out_shape=jax.ShapeDtypeStruct((FIELDS, CYCLES, MODES, LONS), F32),
         scratch_shapes=[
             pltpu.VMEM((DEVS * ROWS, LANES), F32),
             pltpu.VMEM((2, 256, HALF), BF16),
+            pltpu.VMEM((2, 2, FIELDS, CYCLES, MODES, width), F32),
+            pltpu.SemaphoreType.DMA((2, 2)),
         ],
         compiler_params=pltpu.CompilerParams(vmem_limit_bytes=20 << 20),
         name="backward",

time: 89.7 us -> 89.7 us (level)
  waiting for transfers between devices: 7.77 us -> 5.25 us
  local copies, waits for them, and re-layouts: 14 us -> 16.1 us
    all_to_all x1, waiting for transfers between devices: 7.77 us -> 5.25 us  [exchange(): lax.all_to_all(messages, AXES, split_axis=0, concat_axis=0, tiled=True)]
    squeeze x0 -> x1, local copies, waits for them, and re-layouts: none -> 2.17 us  [on_device(): leg[0]]
  transfers between devices with their start and end apart: 1 -> 1, of which waited for: 1 -> 1; matrix products, arithmetic and copies ran while one was open for 16% -> 18% of each run, Pallas kernels for 0% -> 0%
where the time goes in v6:
time: 89.7 us; the launch traced here: 89.4 us
  Pallas kernels  30.4 us (34%)
  blocking collectives  26 us (29%)
  local copies, waits for them, and re-layouts  16.1 us (18%)
  starting transfers between devices  11.6 us (13%)
  waiting for transfers between devices  5.25 us (6%)
    all_to_all x1, blocking collectives, exchange(): lax.all_to_all(messages, AXES, split_axis=0, concat_axis=0, tiled=True)  26 us
    pallas_call x1, Pallas kernels, on_device(): pl.pallas_call(middle_kernel, grid=(SLOTS + 1,), in_specs=[smem, smem, sm...  17.3 us
    all_to_all x1, starting transfers between devices, exchange(): lax.all_to_all(messages, AXES, split_axis=0, concat_axis=0, tiled=True)  11.6 us
    pallas_call x1, Pallas kernels, on_device(): pl.pallas_call(forward_kernel, grid=(SLOTS,), in_specs=[smem, whole((SLOT...  8.27 us
    unnamed x9, local copies, waits for them, and re-layouts  7.01 us
    pad x1, local copies, waits for them, and re-layouts, on_device(): inv = jnp.pad(inv, ((0, 0),) * 6 + ((0, WIDE - COLS),))  6.95 us
    all_to_all x1, waiting for transfers between devices, exchange(): lax.all_to_all(messages, AXES, split_axis=0, concat_axis=0, tiled=True)  5.25 us
    pallas_call x1, Pallas kernels, on_device(): pl.pallas_call(backward_kernel, grid=(HALF // width,), in_specs=[whole((D...  4.74 us
  transfers between devices with their start and end apart: 1, of which 1 were waited for; matrix products, arithmetic and copies ran while one was open for 18% of the time, Pallas kernels for 0%

profile of v6, /device:TPU:0, one launch (start us, length us, event | category | flops | bytes accessed | tf_op | source)
XLA Modules:
  0.0 89.4 jit_solution(14431827898311636421)
XLA Ops:
  0.0 8.3 %forward.1 = (bf16[2,1280,1280]{2,1,0:T(8,128)(2,1)}, bf16[128,40,128]{2,1,0:T(8,128)(2,1)}) custom-call(f32[10]{0:T(128)} %weight_ref.1, s32[5,128]{1,0:T(8,128)} %bitcast.12, bf16[3,10,8,2560]{3,2,1,0:T(8,128)(2,1)} %bitcast.16), custom_call_target="tpu_custom_call" | custom-call | tf_op jit(solution)/shard_map/forward/pallas_call | solution.py:390
  8.3 11.6 %all-to-all-start = ((bf16[128,40,128]{2,1,0:T(8,128)(2,1)}), bf16[128,40,128]{2,1,0:T(8,128)(2,1)}, u32[]{:S(2)}, u32[]{:S(2)}) async-start(bf16[128,40,128]{2,1,0:T(8,128)(2,1)} %get-tuple-element.7), calls=%async_computation | async-start | bytes 2621440 | tf_op jit(solution)/shard_map/all_to_all | solution.py:382
  19.9 7.0 %copy.9 = f32[2,8,5,2,3,3,1281]{6,1,5,4,3,0,2:T(8,128)} copy(f32[2,8,5,2,3,3,1281]{6,3,5,4,2,1,0:T(2,128)} %param.9) | data formatting | bytes 14757120 | tf_op args[3]
  26.9 6.9 %pad.4.inv_hbm = f32[5,2,2,3,3,8,1408]{6,5,4,3,2,1,0:T(8,128)} pad(f32[5,2,2,3,3,8,1281]{6,5,4,3,2,1,0:T(8,128)} %bitcast.13, f32[]{:T(128)} %constant.13.clone.1), padding=0_0x0_0x0_0x0_0x0_0x0_0x0_127 | pad | bytes 15488644 | tf_op jit(solution)/shard_map/jit(_pad)/pad | solution.py:417
  33.9 0.0 copy-start
  33.9 0.0 copy-start.1
  33.9 2.2 %slice_bitcast_fusion.leg_first = bf16[1281,1280]{1,0:T(8,128)(2,1)S(1)} fusion(bf16[5,1281,1280]{2,1,0:T(8,128)(2,1)} %bitcast.14), kind=kLoop, calls=%fused_computation.1 | loop fusion | bytes 6558720 | tf_op jit(solution)/shard_map/squeeze | solution.py:447
  36.0 5.3 %all-to-all-done.recv_ref = bf16[128,40,128]{2,1,0:T(8,128)(2,1)} async-done(((bf16[128,40,128]{2,1,0:T(8,128)(2,1)}), bf16[128,40,128]{2,1,0:T(8,128)(2,1)}, u32[]{:S(2)}, u32[]{:S(2)}) %all-to-all-start) | async-done | bytes 1310752 | tf_op jit(solution)/shard_map/all_to_all | solution.py:382
  41.3 0.0 slice-start
  41.3 0.0 copy-done
  41.3 0.0 copy-done.1
  41.3 0.0 slice-start.1
  41.3 17.3 %middle.1 = bf16[128,40,128]{2,1,0:T(8,128)(2,1)S(1)} custom-call(s32[1]{0:T(128)} %bitcast.owner_ref, s32[640]{0:T(1024)S(1)} %copy-done, f32[2,2]{1,0:T(2,128)S(1)} %copy-done.1, bf16[128,40,128]{2,1,0:T(8,128)(2,1)} %all-to-all-done.recv_ref, bf16[1281,1280]{1,0:T(8,128)(2,1)S(1)} %slice_bitcast_fusion.leg_first, bf16[5,1281,1280]{2,1,0:T(8,128)(2,1)} %bitcast.15, ...), custom_call_target="tpu_custom_call" | custom-call | tf_op jit(solution)/shard_map/middle/pallas_call | solution.py:420
  58.7 26.0 %all_to_all.10.recv_ref = bf16[128,40,128]{2,1,0:T(8,128)(2,1)S(1)} all-to-all(bf16[128,40,128]{2,1,0:T(8,128)(2,1)S(1)} %middle.1), channel_id=1, replica_groups=mesh['pole'=8,'lat'=16] {'pole','lat'}, dimensions={0} | all-to-all | bytes 2621440 | tf_op jit(solution)/shard_map/all_to_all | solution.py:382
  84.7 0.0 slice-done
  84.7 0.0 slice-done.1
  84.7 4.7 %backward.1 = f32[3,10,8,2560]{3,2,1,0:T(8,128)} custom-call(bf16[128,40,128]{2,1,0:T(8,128)(2,1)S(1)} %all_to_all.10.recv_ref, bf16[2,1280,1280]{2,1,0:T(8,128)(2,1)S(1)} %bitcast.11), custom_call_target="tpu_custom_call" | custom-call | tf_op jit(solution)/shard_map/backward/pallas_call | solution.py:452
  (1 shorter events, 0.0 us)
Async XLA Ops:
  8.3 33.0 %all-to-all-start = ((bf16[128,40,128]{2,1,0:T(8,128)(2,1)}), bf16[128,40,128]{2,1,0:T(8,128)(2,1)}, u32[]{:S(2)}, u32[]{:S(2)}) async-start(bf16[128,40,128]{2,1,0:T(8,128)(2,1)} %get-tuple-element.7), calls=%async_computation | async-start | bytes 2621440 | tf_op jit(solution)/shard_map/all_to_all | solution.py:382
  33.9 7.4 %copy-start = (s32[640]{0:T(1024)S(1)}, s32[640]{0:T(1024)}, u32[]{:S(2)}) copy-start(s32[640]{0:T(1024)} %pair_ref.1) | copy-start | bytes 7684
  33.9 7.4 %copy-start.1 = (f32[2,2]{1,0:T(2,128)S(1)}, f32[2,2]{1,0:T(2,128)}, u32[]{:S(2)}) copy-start(f32[2,2]{1,0:T(2,128)} %pole_ref.1) | copy-start | bytes 52
  41.3 43.4 %slice-start = ((s8[6553600]{0:T(1024)(128)(4,1)}), s8[4194304]{0:T(1024)(128)(4,1)S(1)}, s32[]{:S(2)}) async-start(s8[6553600]{0:T(1024)(128)(4,1)} %bitcast.10), calls=%async_computation.2 | async-start | bytes 8388608
  41.3 43.4 %slice-start.1 = ((s8[6553600]{0:T(1024)(128)(4,1)}), s8[2359296]{0:T(1024)(128)(4,1)S(1)}, s32[]{:S(2)}) async-start(s8[6553600]{0:T(1024)(128)(4,1)} %bitcast.10), calls=%async_computation.3 | async-start | bytes 4718592

commit v7 on v6

--- a/solution.py
+++ b/solution.py
@@ -247,16 +247,13 @@
 
 
 def middle_kernel(
-    owner_ref, pair_ref, pole_ref, recv_ref, leg_first, leg_hbm, inv_hbm, send_ref,
+    owner_ref, pair_ref, pole_ref, recv_ref, leg_hbm, inv_hbm, send_ref,
     leg_scr, inv_scr, spec_scr, pack_in, cycle_in, pack_out, cycle_out, leg_sem, inv_sem,
 ):
     step = pl.program_id(0)
 
     def leg_copy(slot):
         return pltpu.make_async_copy(leg_hbm.at[slot], leg_scr.at[slot], leg_sem.at[slot])
-
-    def first_copy():
-        return pltpu.make_async_copy(leg_first, leg_scr.at[0], leg_sem.at[0])
 
     def inv_copy(slot):
         return pltpu.make_async_copy(inv_hbm.at[slot], inv_scr.at[slot], inv_sem.at[slot])
@@ -277,11 +274,11 @@
 
     @pl.when(step == 0)
     def _():
-        first_copy().start()
+        leg_copy(0).start()
         inv_copy(0).start()
         leg_copy(1).start()
         column = unpack_columns(recv_ref, pack_in, cycle_in)
-        first_copy().wait()
+        leg_copy(0).wait()
         inv_copy(1).start()
         leg_copy(2).start()
         store_spec(*analyse(column, leg_scr.at[0]))
@@ -425,7 +422,6 @@
             smem,
             smem,
             pl.BlockSpec((DEVS, SUB, LANES), lambda i: (0, jnp.minimum(i, SLOTS - 1), 0)),
-            anywhere,
             anywhere,
             anywhere,
         ],
@@ -442,9 +438,9 @@
             pltpu.SemaphoreType.DMA((SLOTS,)),
             pltpu.SemaphoreType.DMA((SLOTS,)),
         ],
-        compiler_params=pltpu.CompilerParams(vmem_limit_bytes=46 << 20),
+        compiler_params=pltpu.CompilerParams(vmem_limit_bytes=50 << 20),
         name="middle",
-    )(owner, pair_order, pole_coeffs, incoming, leg[0], leg, inv)
+    )(owner, pair_order, pole_coeffs, incoming, leg, inv)
 
     back = exchange(returning)
 

time: 89.7 us -> 89.3 us (level)
  waiting for transfers between devices: 5.25 us -> 7.77 us
  local copies, waits for them, and re-layouts: 16.1 us -> 14 us
    all_to_all x1, waiting for transfers between devices: 5.25 us -> 7.77 us  [exchange(): lax.all_to_all(messages, AXES, split_axis=0, concat_axis=0, tiled=True)]
    squeeze x1 -> x0, local copies, waits for them, and re-layouts: 2.17 us -> none  [on_device(): leg[0]]
  transfers between devices with their start and end apart: 1 -> 1, of which waited for: 1 -> 1; matrix products, arithmetic and copies ran while one was open for 18% -> 16% of each run, Pallas kernels for 0% -> 0%
where the time goes in v7:
time: 89.3 us; the launch traced here: 89 us
  Pallas kernels  30.3 us (34%)
  blocking collectives  25.7 us (29%)
  local copies, waits for them, and re-layouts  14 us (16%)
  starting transfers between devices  11.2 us (13%)
  waiting for transfers between devices  7.77 us (9%)
    all_to_all x1, blocking collectives, exchange(): lax.all_to_all(messages, AXES, split_axis=0, concat_axis=0, tiled=True)  25.7 us
    pallas_call x1, Pallas kernels, on_device(): pl.pallas_call(middle_kernel, grid=(SLOTS + 1,), in_specs=[smem, smem, sm...  17.3 us
    all_to_all x1, starting transfers between devices, exchange(): lax.all_to_all(messages, AXES, split_axis=0, concat_axis=0, tiled=True)  11.2 us
    pallas_call x1, Pallas kernels, on_device(): pl.pallas_call(forward_kernel, grid=(SLOTS,), in_specs=[smem, whole((SLOT...  8.27 us
    all_to_all x1, waiting for transfers between devices, exchange(): lax.all_to_all(messages, AXES, split_axis=0, concat_axis=0, tiled=True)  7.77 us
    pad x1, local copies, waits for them, and re-layouts, on_device(): inv = jnp.pad(inv, ((0, 0),) * 6 + ((0, WIDE - COLS),))  7.02 us
    unnamed x9, local copies, waits for them, and re-layouts  6.96 us
    pallas_call x1, Pallas kernels, on_device(): pl.pallas_call(backward_kernel, grid=(HALF // width,), in_specs=[whole((D...  4.74 us
  transfers between devices with their start and end apart: 1, of which 1 were waited for; matrix products, arithmetic and copies ran while one was open for 16% of the time, Pallas kernels for 0%

profile of v7, /device:TPU:0, one launch (start us, length us, event | category | flops | bytes accessed | tf_op | source)
XLA Modules:
  0.0 89.0 jit_solution(14984102381939609105)
XLA Ops:
  0.0 8.3 %forward.1 = (bf16[2,1280,1280]{2,1,0:T(8,128)(2,1)}, bf16[128,40,128]{2,1,0:T(8,128)(2,1)}) custom-call(f32[10]{0:T(128)} %weight_ref.1, s32[5,128]{1,0:T(8,128)} %bitcast.10, bf16[3,10,8,2560]{3,2,1,0:T(8,128)(2,1)} %bitcast.13), custom_call_target="tpu_custom_call" | custom-call | tf_op jit(solution)/shard_map/forward/pallas_call | solution.py:387
  8.3 11.2 %all-to-all-start = ((bf16[128,40,128]{2,1,0:T(8,128)(2,1)}), bf16[128,40,128]{2,1,0:T(8,128)(2,1)S(1)}, u32[]{:S(2)}, u32[]{:S(2)}) async-start(bf16[128,40,128]{2,1,0:T(8,128)(2,1)} %get-tuple-element.7), calls=%async_computation | async-start | bytes 2621440 | tf_op jit(solution)/shard_map/all_to_all | solution.py:379
  19.5 6.9 %copy.9 = f32[2,8,5,2,3,3,1281]{6,1,5,4,3,0,2:T(8,128)} copy(f32[2,8,5,2,3,3,1281]{6,3,5,4,2,1,0:T(2,128)} %param.9) | data formatting | bytes 14757120 | tf_op args[3]
  26.4 0.0 copy-start
  26.4 0.0 copy-start.1
  26.4 7.0 %pad.4.inv_hbm = f32[5,2,2,3,3,8,1408]{6,5,4,3,2,1,0:T(8,128)} pad(f32[5,2,2,3,3,8,1281]{6,5,4,3,2,1,0:T(8,128)} %bitcast.11, f32[]{:T(128)} %constant.13.clone.1), padding=0_0x0_0x0_0x0_0x0_0x0_0x0_127 | pad | bytes 15488644 | tf_op jit(solution)/shard_map/jit(_pad)/pad | solution.py:414
  33.4 7.8 %all-to-all-done.recv_ref = bf16[128,40,128]{2,1,0:T(8,128)(2,1)S(1)} async-done(((bf16[128,40,128]{2,1,0:T(8,128)(2,1)}), bf16[128,40,128]{2,1,0:T(8,128)(2,1)S(1)}, u32[]{:S(2)}, u32[]{:S(2)}) %all-to-all-start) | async-done | bytes 1310752 | tf_op jit(solution)/shard_map/all_to_all | solution.py:379
  41.2 0.0 slice-start
  41.2 0.0 copy-done
  41.2 0.0 copy-done.1
  41.2 0.0 slice-start.1
  41.2 17.3 %middle.1 = bf16[128,40,128]{2,1,0:T(8,128)(2,1)S(1)} custom-call(s32[1]{0:T(128)} %bitcast.owner_ref, s32[640]{0:T(1024)S(1)} %copy-done, f32[2,2]{1,0:T(2,128)S(1)} %copy-done.1, bf16[128,40,128]{2,1,0:T(8,128)(2,1)S(1)} %all-to-all-done.recv_ref, bf16[5,1281,1280]{2,1,0:T(8,128)(2,1)} %bitcast.12, f32[5,2,2,3,3,8,1408]{6,5,4,3,2,1,0:T(8,128)} %pad.4.inv_hbm), custom_call_target="tpu_custom_call" | custom-call | tf_op jit(solution)/shard_map/middle/pallas_call | solution.py:417
  58.5 25.7 %all_to_all.10.recv_ref = bf16[128,40,128]{2,1,0:T(8,128)(2,1)S(1)} all-to-all(bf16[128,40,128]{2,1,0:T(8,128)(2,1)S(1)} %middle.1), channel_id=1, replica_groups=mesh['pole'=8,'lat'=16] {'pole','lat'}, dimensions={0} | all-to-all | bytes 2621440 | tf_op jit(solution)/shard_map/all_to_all | solution.py:379
  84.2 0.0 slice-done
  84.2 0.0 slice-done.1
  84.3 4.7 %backward.1 = f32[3,10,8,2560]{3,2,1,0:T(8,128)} custom-call(bf16[128,40,128]{2,1,0:T(8,128)(2,1)S(1)} %all_to_all.10.recv_ref, bf16[2,1280,1280]{2,1,0:T(8,128)(2,1)S(1)} %bitcast.9), custom_call_target="tpu_custom_call" | custom-call | tf_op jit(solution)/shard_map/backward/pallas_call | solution.py:448
  (1 shorter events, 0.0 us)
Async XLA Ops:
  8.3 32.9 %all-to-all-start = ((bf16[128,40,128]{2,1,0:T(8,128)(2,1)}), bf16[128,40,128]{2,1,0:T(8,128)(2,1)S(1)}, u32[]{:S(2)}, u32[]{:S(2)}) async-start(bf16[128,40,128]{2,1,0:T(8,128)(2,1)} %get-tuple-element.7), calls=%async_computation | async-start | bytes 2621440 | tf_op jit(solution)/shard_map/all_to_all | solution.py:379
  26.4 14.8 %copy-start = (s32[640]{0:T(1024)S(1)}, s32[640]{0:T(1024)}, u32[]{:S(2)}) copy-start(s32[640]{0:T(1024)} %pair_ref.1) | copy-start | bytes 7684
  26.4 14.8 %copy-start.1 = (f32[2,2]{1,0:T(2,128)S(1)}, f32[2,2]{1,0:T(2,128)}, u32[]{:S(2)}) copy-start(f32[2,2]{1,0:T(2,128)} %pole_ref.1) | copy-start | bytes 52
  41.2 43.1 %slice-start = ((s8[6553600]{0:T(1024)(128)(4,1)}), s8[4194304]{0:T(1024)(128)(4,1)S(1)}, s32[]{:S(2)}) async-start(s8[6553600]{0:T(1024)(128)(4,1)} %bitcast.8), calls=%async_computation.2 | async-start | bytes 8388608
  41.2 43.0 %slice-start.1 = ((s8[6553600]{0:T(1024)(128)(4,1)}), s8[2359296]{0:T(1024)(128)(4,1)S(1)}, s32[]{:S(2)}) async-start(s8[6553600]{0:T(1024)(128)(4,1)} %bitcast.8), calls=%async_computation.3 | async-start | bytes 4718592
